TPU v7x, 768 devices: a whole 4x8x12 slice. The times are simulated.
768 devices in a mesh: outer: 24 (over x_hi, z), inner: 16 (over y, core), head: 2 (over x_lo).
Axes of the slice: x: 4 (x_hi: 2, x_lo: 2; x = x_hi * 2 + x_lo), y: 8, z: 12, core: 2. Of those that a mesh axis runs over, the one named last changes fastest.
Arguments:
- queries: bfloat16 [49152, 8, 1024], P(('outer', 'inner'), 'head'), may hold values from -7 to 7
- keys: bfloat16 [49152, 1024], P(('outer', 'inner')), may hold values from -4 to 4
- values: bfloat16 [49152, 1024], P(('outer', 'inner')), may hold values from -6 to 6
- grad_out: bfloat16 [49152, 8, 1024], P(('outer', 'inner'), 'head'), may hold values from -6 to 6
- positions: int32 [49152], P(('outer', 'inner')), may hold values from 0 to 18431, as said below
Outputs:
- grad_queries: bfloat16 [49152, 8, 1024], P(('outer', 'inner'), 'head')
- grad_keys: bfloat16 [49152, 1024], P(('outer', 'inner'), 'head')
- grad_values: bfloat16 [49152, 1024], P(('outer', 'inner'), 'head')
Inputs may be any that keep to these rules, and one draw needn't show every extreme that they name: `positions`: time ids never fall along the sequence; every id is held by 2 to 4 consecutive tokens.
All inputs are finite; a program needn't handle non-finite values.
Results may differ from a plain program's by a relative error of at most 0.0055.
The roundings to bfloat16 on the way count: a program that leaves them out, or rounds other values in their place, can miss the bound.
Values may be sent and summed in bfloat16 or wider, within the bound.
A program may use at most 64 MiB of HBM per device.

v0:
```python
import math

import jax
import jax.numpy as jnp
import numpy as np
from jax import lax
from jax.sharding import PartitionSpec as P

HEAD = 128
WINDOW_BLOCKS = 4


rope_theta = 500000.0
rope_factor = 128.0
initial_context = 8192.0
ramp_low = 1.0
ramp_high = 32.0
attention_factor = 1.0 + 0.1 * math.log(rope_factor)


def from_behind(value, axis, steps):
    count = lax.axis_size(axis)
    first, last = (max(0, -steps), min(count, count - steps))
    return lax.ppermute(value, axis, [(source, source + steps) for source in range(first, last)])


def yarn_frequencies():
    halves = HEAD // 2
    powers = rope_theta ** (-2.0 * np.arange(halves) / HEAD)
    turns = initial_context * powers / (2.0 * np.pi)
    blend = np.clip((turns - ramp_low) / (ramp_high - ramp_low), 0.0, 1.0)
    return jnp.asarray(powers * ((1.0 - blend) / rope_factor + blend), jnp.float32)


def rope_tables(positions):
    frequency = yarn_frequencies()
    angles = positions.astype(jnp.float32)[:, None] * frequency[None, :]
    return (attention_factor * jnp.cos(angles), attention_factor * jnp.sin(angles))


def rotate(vector, cosines, sines):
    middle = vector.shape[-1] // 2
    leading = vector[..., :middle]
    trailing = vector[..., middle:]
    return jnp.concatenate(
        [leading * cosines - trailing * sines, trailing * cosines + leading * sines], -1
    )


def unrotate(vector, cosines, sines):
    middle = vector.shape[-1] // 2
    leading = vector[..., :middle]
    trailing = vector[..., middle:]
    return jnp.concatenate(
        [leading * cosines + trailing * sines, trailing * cosines - leading * sines], -1
    )


def forward(key_value, distance):
    arrived = from_behind(key_value, ("outer", "inner"), distance)
    return arrived


def backward(partial_value, distance):
    arrived = from_behind(partial_value, ("outer", "inner"), -distance)
    return arrived


def body(queries, keys, values, grad_out, positions):
    local_rows = keys.shape[0]
    score_scale = 1.0 / math.sqrt(HEAD)
    query_local, grad_local = (queries, grad_out)
    key_local, value_local = (keys, values)
    groups = query_local.shape[1]
    columns = query_local.shape[2]
    heads_here = columns // HEAD
    cosines, sines = rope_tables(positions)
    rotated_queries = rotate(
        query_local.reshape(local_rows, groups, heads_here, HEAD).astype(jnp.float32),
        cosines[:, None, None, :],
        sines[:, None, None, :],
    ).astype(jnp.bfloat16)
    rotated_keys = rotate(
        key_local.reshape(local_rows, heads_here, HEAD).astype(jnp.float32),
        cosines[:, None, :],
        sines[:, None, :],
    ).astype(jnp.bfloat16)
    key_value = jnp.stack([rotated_keys.reshape(local_rows, columns), value_local], 0)
    received = [key_value]
    for distance in range(1, WINDOW_BLOCKS + 1):
        received.append(forward(key_value, distance))
    window = jnp.concatenate(received[::-1], 1)
    window_len = window.shape[1]
    behind = window_len - local_rows
    window_heads = window.reshape(2, window_len, heads_here, HEAD).transpose(2, 0, 1, 3)
    query_heads = rotated_queries.transpose(2, 1, 0, 3)
    grad_heads = grad_local.reshape(local_rows, groups, heads_here, HEAD).transpose(2, 1, 0, 3)
    offset = lax.axis_index(("outer", "inner")) * local_rows
    query_ids = jnp.arange(local_rows, dtype=jnp.int32)[:, None]
    window_ids = jnp.arange(window_len, dtype=jnp.int32)[None, :]
    allowed = (
        (window_ids > query_ids)
        & (window_ids <= query_ids + behind)
        & (offset - behind + window_ids >= 0)
    )
    row_total = groups * local_rows
    inner_dims = (((1,), (1,)), ((), ()))
    outer_dims = (((0,), (0,)), ((), ()))

    def per_head(operands):
        query_part, grad_part, window_part = operands
        query_rows = query_part.reshape(row_total, HEAD)
        grad_rows = grad_part.reshape(row_total, HEAD)
        scores = (
            lax.dot_general(
                query_rows, window_part[0], inner_dims, preferred_element_type=jnp.float32
            )
            * score_scale
        )
        scores = jnp.where(allowed[None], scores.reshape(groups, local_rows, window_len), -jnp.inf)
        row_max = jnp.max(scores, -1, keepdims=True)
        raised = jnp.exp(scores - row_max)
        weights = raised / jnp.sum(raised, -1, keepdims=True)
        weights_low = weights.astype(jnp.bfloat16).reshape(row_total, window_len)
        weight_grads = lax.dot_general(
            grad_rows, window_part[1], inner_dims, preferred_element_type=jnp.float32
        ).reshape(groups, local_rows, window_len)
        row_terms = jnp.sum(weights * weight_grads, -1, keepdims=True)
        score_grads = (
            (weights * (weight_grads - row_terms))
            .astype(jnp.bfloat16)
            .reshape(row_total, window_len)
        )
        query_grads = (
            jnp.dot(score_grads, window_part[0], preferred_element_type=jnp.float32) * score_scale
        )
        key_part = (
            lax.dot_general(score_grads, query_rows, outer_dims, preferred_element_type=jnp.float32)
            * score_scale
        )
        value_part = lax.dot_general(
            weights_low, grad_rows, outer_dims, preferred_element_type=jnp.float32
        )
        return (query_grads, jnp.stack([key_part, value_part], 0))

    query_grads, pair_grads = lax.map(per_head, (query_heads, grad_heads, window_heads))
    query_grads = query_grads.reshape(heads_here, groups, local_rows, HEAD).transpose(2, 1, 0, 3)
    query_result = (
        unrotate(query_grads, cosines[:, None, None, :], sines[:, None, None, :])
        .astype(jnp.bfloat16)
        .reshape(local_rows, groups, columns)
    )
    partials = pair_grads.transpose(1, 2, 0, 3).reshape(2, WINDOW_BLOCKS + 1, local_rows, columns)
    summed = partials[:, WINDOW_BLOCKS]
    for distance in range(1, WINDOW_BLOCKS + 1):
        summed = summed + backward(partials[:, WINDOW_BLOCKS - distance], distance)
    owned = lax.psum_scatter(summed, "head", scatter_dimension=2, tiled=True)
    owned_heads = owned.shape[2] // HEAD
    grad_keys = (
        unrotate(
            owned[0].reshape(local_rows, owned_heads, HEAD), cosines[:, None, :], sines[:, None, :]
        )
        .astype(jnp.bfloat16)
        .reshape(local_rows, owned_heads * HEAD)
    )
    grad_values = owned[1].astype(jnp.bfloat16)
    return (query_result, grad_keys, grad_values)


def solution(mesh):
    placed = (
        P(("outer", "inner"), "head", None),
        P(("outer", "inner"), None),
        P(("outer", "inner"), None),
        P(("outer", "inner"), "head", None),
        P(("outer", "inner")),
    )
    return jax.shard_map(
        body,
        mesh=mesh,
        in_specs=placed,
        out_specs=(
            P(("outer", "inner"), "head", None),
            P(("outer", "inner"), "head"),
            P(("outer", "inner"), "head"),
        ),
        check_vma=False,
    )
```

profile of v0, /device:TPU:1, one launch (start us, length us, event | category | flops | bytes accessed | tf_op | source)
XLA Modules:
  0.0 355.2 jit_solution(335881753670808367)
XLA Ops:
  11.2 5.9 %collective-permute-start = (bf16[2,128,1024]{1,2,0:T(8,128)(2,1)S(1)}, bf16[2,128,1024]{1,2,0:T(8,128)(2,1)}, u32[]{:S(2)}, u32[]{:S(2)}) collective-permute-start(bf16[2,128,1024]{1,2,0:T(8,128)(2,1)S(1)} %pad_maximum_fusion.1), channel_id=1, source_target_pairs={{0,8},{2,10},{4,12},{6,14},{8,16},{10,18},{12,20},{14,22},{16,24},... | collective-permute-start | bytes 1572872 | tf_op jit(solution)/shard_map/ppermute | solution.py:24
  17.1 6.3 %collective-permute-start.1 = (bf16[2,128,1024]{1,2,0:T(8,128)(2,1)S(1)}, bf16[2,128,1024]{1,2,0:T(8,128)(2,1)}, u32[]{:S(2)}, u32[]{:S(2)}) collective-permute-start(bf16[2,128,1024]{1,2,0:T(8,128)(2,1)S(1)} %pad_maximum_fusion.1), channel_id=1, source_target_pairs={{0,6},{2,8},{4,10},{6,12},{8,14},{10,16},{12,18},{14,20},{16,22},{... | collective-permute-start | bytes 1572872 | tf_op jit(solution)/shard_map/ppermute | solution.py:24
  33.9 4.5 %collective-permute-done.1 = bf16[2,128,1024]{1,2,0:T(8,128)(2,1)} collective-permute-done((bf16[2,128,1024]{1,2,0:T(8,128)(2,1)S(1)}, bf16[2,128,1024]{1,2,0:T(8,128)(2,1)}, u32[]{:S(2)}, u32[]{:S(2)}) %collective-permute-start.1) | collective-permute-done | bytes 524320 | tf_op jit(solution)/shard_map/ppermute | solution.py:24
  39.6 18.7 %collective-permute-done.2 = bf16[2,128,1024]{1,2,0:T(8,128)(2,1)} collective-permute-done((bf16[2,128,1024]{1,2,0:T(8,128)(2,1)S(1)}, bf16[2,128,1024]{1,2,0:T(8,128)(2,1)}, u32[]{:S(2)}, u32[]{:S(2)}) %collective-permute-start.2) | collective-permute-done | bytes 524320 | tf_op jit(solution)/shard_map/ppermute | solution.py:24
  59.4 13.5 %collective-permute-done.3 = bf16[2,128,1024]{1,2,0:T(8,128)(2,1)} collective-permute-done((bf16[2,128,1024]{1,2,0:T(8,128)(2,1)S(1)}, bf16[2,128,1024]{1,2,0:T(8,128)(2,1)}, u32[]{:S(2)}, u32[]{:S(2)}) %collective-permute-start.3) | collective-permute-done | bytes 524320 | tf_op jit(solution)/shard_map/ppermute | solution.py:24
  75.8 92.2 %while.13 = (s32[]{:T(128)}, f32[8,512,128]{2,1,0:T(8,128)}, f32[8,2,640,128]{3,2,1,0:T(8,128)}, bf16[8,4,128,128]{2,3,0,1:T(8,128)(2,1)}, bf16[8,2,640,128]{2,3...) while((s32[]{:T(128)}, f32[8,512,128]{2,1,0:T(8,128)}, ...), condition=%wide.region_4.5_spmd.clone, body=%wide.region_0.4_spmd.clone.sunk | while | flops 426623104 | bytes 15862017 | solution.py:146
  81.1 3.0 fusion.62
  92.6 3.0 fusion.62
  104.1 3.0 fusion.62
  115.7 3.0 fusion.62
  127.2 3.0 fusion.62
  138.7 3.0 fusion.62
  150.2 3.0 fusion.62
  161.8 3.0 fusion.62
  168.0 7.9 %copy.35 = f32[2,640,8,128]{3,2,1,0:T(8,128)} copy(f32[2,640,8,128]{3,1,0,2:T(8,128)} %bitcast.156) | data formatting | bytes 10485760 | tf_op jit(solution)/shard_map/transpose | solution.py:153
  175.9 6.7 %reshape.182 = f32[2,5,128,1024]{3,2,1,0:T(8,128)} reshape(f32[2,640,8,128]{3,2,1,0:T(8,128)} %copy.35) | data formatting | bytes 10485760 | tf_op jit(solution)/shard_map/reshape | solution.py:153
  182.6 2.5 slice_bitcast_fusion.3
  185.1 4.1 %collective-permute-start.4 = (f32[2,128,1024]{2,1,0:T(8,128)S(1)}, f32[2,128,1024]{2,1,0:T(8,128)S(1)}, u32[]{:S(2)}, u32[]{:S(2)}) collective-permute-start(f32[2,128,1024]{2,1,0:T(8,128)S(1)} %get-tuple-element.105), channel_id=1, source_target_pairs={{2,0},{4,2},{6,4},{8,6},{10,8},{12,10},{14,12},{16,14},{18,16},{20... | collective-permute-start | bytes 3145736 | tf_op jit(solution)/shard_map/ppermute | solution.py:24
  193.3 31.6 %collective-permute-done.4 = f32[2,128,1024]{2,1,0:T(8,128)S(1)} collective-permute-done((f32[2,128,1024]{2,1,0:T(8,128)S(1)}, f32[2,128,1024]{2,1,0:T(8,128)S(1)}, u32[]{:S(2)}, u32[]{:S(2)}) %collective-permute-start.4) | collective-permute-done | bytes 1048608 | tf_op jit(solution)/shard_map/ppermute | solution.py:24
  224.9 8.1 %collective-permute-done.5 = f32[2,128,1024]{2,1,0:T(8,128)S(1)} collective-permute-done((f32[2,128,1024]{2,1,0:T(8,128)S(1)}, f32[2,128,1024]{2,1,0:T(8,128)S(1)}, u32[]{:S(2)}, u32[]{:S(2)}) %collective-permute-start.5) | collective-permute-done | bytes 1048608 | tf_op jit(solution)/shard_map/ppermute | solution.py:24
  232.9 56.0 %collective-permute-done.6 = f32[2,128,1024]{2,1,0:T(8,128)S(1)} collective-permute-done((f32[2,128,1024]{2,1,0:T(8,128)S(1)}, f32[2,128,1024]{2,1,0:T(8,128)S(1)}, u32[]{:S(2)}, u32[]{:S(2)}) %collective-permute-start.6) | collective-permute-done | bytes 1048608 | tf_op jit(solution)/shard_map/ppermute | solution.py:24
  289.0 8.0 %collective-permute-done.7 = f32[2,128,1024]{2,1,0:T(8,128)S(1)} collective-permute-done((f32[2,128,1024]{2,1,0:T(8,128)S(1)}, f32[2,128,1024]{2,1,0:T(8,128)S(1)}, u32[]{:S(2)}, u32[]{:S(2)}) %collective-permute-start.7) | collective-permute-done | bytes 1048608 | tf_op jit(solution)/shard_map/ppermute | solution.py:24
  297.0 2.8 fusion.24
  304.0 40.5 %reduce-scatter.2.cloned.1.call-done = f32[2,128,512]{2,1,0:T(8,128)} async-done(((f32[2,128,1024]{2,1,0:T(8,128)}), f32[2,128,512]{2,1,0:T(8,128)}) %reduce-scatter.2.cloned.1.call-update) | async-done | bytes 524304 | tf_op jit(solution)/shard_map/reduce_scatter | solution.py:157
  (143 shorter events, 99.7 us)
Async XLA Ops:
  7.2 20.4 %copy-start.1 = (bf16[128,4,1024]{2,1,0:T(4,128)(2,1)S(1)}, bf16[128,4,1024]{2,1,0:T(4,128)(2,1)}, u32[]{:S(2)}) copy-start(bf16[128,4,1024]{2,1,0:T(4,128)(2,1)} %param.8) | copy-start | bytes 3145732
  7.2 337.3 %reduce-scatter.2.cloned.1.call-start = ((), (), s32[]{:S(2)}) async-start(), calls=%async_computation.1 | async-start | bytes 1572864 | tf_op jit(solution)/shard_map/reduce_scatter | solution.py:157
  11.2 21.6 %collective-permute-start = (bf16[2,128,1024]{1,2,0:T(8,128)(2,1)S(1)}, bf16[2,128,1024]{1,2,0:T(8,128)(2,1)}, u32[]{:S(2)}, u32[]{:S(2)}) collective-permute-start(bf16[2,128,1024]{1,2,0:T(8,128)(2,1)S(1)} %pad_maximum_fusion.1), channel_id=1, source_target_pairs={{0,8},{2,10},{4,12},{6,14},{8,16},{10,18},{12,20},{14,22},{16,24},... | collective-permute-start | bytes 1572872 | tf_op jit(solution)/shard_map/ppermute | solution.py:24
  17.1 21.4 %collective-permute-start.1 = (bf16[2,128,1024]{1,2,0:T(8,128)(2,1)S(1)}, bf16[2,128,1024]{1,2,0:T(8,128)(2,1)}, u32[]{:S(2)}, u32[]{:S(2)}) collective-permute-start(bf16[2,128,1024]{1,2,0:T(8,128)(2,1)S(1)} %pad_maximum_fusion.1), channel_id=1, source_target_pairs={{0,6},{2,8},{4,10},{6,12},{8,14},{10,16},{12,18},{14,20},{16,22},{... | collective-permute-start | bytes 1572872 | tf_op jit(solution)/shard_map/ppermute | solution.py:24
  23.3 34.9 %collective-permute-start.2 = (bf16[2,128,1024]{1,2,0:T(8,128)(2,1)S(1)}, bf16[2,128,1024]{1,2,0:T(8,128)(2,1)}, u32[]{:S(2)}, u32[]{:S(2)}) collective-permute-start(bf16[2,128,1024]{1,2,0:T(8,128)(2,1)S(1)} %pad_maximum_fusion.1), channel_id=1, source_target_pairs={{0,4},{2,6},{4,8},{6,10},{8,12},{10,14},{12,16},{14,18},{16,20},{1... | collective-permute-start | bytes 1572872 | tf_op jit(solution)/shard_map/ppermute | solution.py:24
  25.6 47.3 %collective-permute-start.3 = (bf16[2,128,1024]{1,2,0:T(8,128)(2,1)S(1)}, bf16[2,128,1024]{1,2,0:T(8,128)(2,1)}, u32[]{:S(2)}, u32[]{:S(2)}) collective-permute-start(bf16[2,128,1024]{1,2,0:T(8,128)(2,1)S(1)} %pad_maximum_fusion.1), channel_id=1, source_target_pairs={{0,2},{2,4},{4,6},{6,8},{8,10},{10,12},{12,14},{14,16},{16,18},{18... | collective-permute-start | bytes 1572872 | tf_op jit(solution)/shard_map/ppermute | solution.py:24
  28.8 1.2 copy-start.2
  74.3 1.5 copy-start
  185.1 39.8 %collective-permute-start.4 = (f32[2,128,1024]{2,1,0:T(8,128)S(1)}, f32[2,128,1024]{2,1,0:T(8,128)S(1)}, u32[]{:S(2)}, u32[]{:S(2)}) collective-permute-start(f32[2,128,1024]{2,1,0:T(8,128)S(1)} %get-tuple-element.105), channel_id=1, source_target_pairs={{2,0},{4,2},{6,4},{8,6},{10,8},{12,10},{14,12},{16,14},{18,16},{20... | collective-permute-start | bytes 3145736 | tf_op jit(solution)/shard_map/ppermute | solution.py:24
  189.2 43.7 %collective-permute-start.5 = (f32[2,128,1024]{2,1,0:T(8,128)S(1)}, f32[2,128,1024]{2,1,0:T(8,128)S(1)}, u32[]{:S(2)}, u32[]{:S(2)}) collective-permute-start(f32[2,128,1024]{2,1,0:T(8,128)S(1)} %get-tuple-element.106), channel_id=1, source_target_pairs={{4,0},{6,2},{8,4},{10,6},{12,8},{14,10},{16,12},{18,14},{20,16},{2... | collective-permute-start | bytes 3145736 | tf_op jit(solution)/shard_map/ppermute | solution.py:24
  190.5 98.5 %collective-permute-start.6 = (f32[2,128,1024]{2,1,0:T(8,128)S(1)}, f32[2,128,1024]{2,1,0:T(8,128)S(1)}, u32[]{:S(2)}, u32[]{:S(2)}) collective-permute-start(f32[2,128,1024]{2,1,0:T(8,128)S(1)} %get-tuple-element.108), channel_id=1, source_target_pairs={{6,0},{8,2},{10,4},{12,6},{14,8},{16,10},{18,12},{20,14},{22,16},{... | collective-permute-start | bytes 3145736 | tf_op jit(solution)/shard_map/ppermute | solution.py:24
  191.8 105.2 %collective-permute-start.7 = (f32[2,128,1024]{2,1,0:T(8,128)S(1)}, f32[2,128,1024]{2,1,0:T(8,128)S(1)}, u32[]{:S(2)}, u32[]{:S(2)}) collective-permute-start(f32[2,128,1024]{2,1,0:T(8,128)S(1)} %get-tuple-element.107), channel_id=1, source_target_pairs={{8,0},{10,2},{12,4},{14,6},{16,8},{18,10},{20,12},{22,14},{24,16},... | collective-permute-start | bytes 3145736 | tf_op jit(solution)/shard_map/ppermute | solution.py:24
Sparse Core Ops, SparseCore 0:
  299.9 44.5 reduce-scatter.1
where the time goes:
time: 357 us; the launch traced here: 355 us
  waiting for transfers between devices  181 us (51%)
  local copies, waits for them, and re-layouts  46.1 us (13%)
  other arithmetic  45.6 us (13%)
  matrix products  43.4 us (12%)
  starting transfers between devices  24.6 us (7%)
  between operations  14.3 us (4%)
    ppermute x8, waiting for transfers between devices, from_behind(): lax.ppermute(value, axis, [(source, source + steps) for source in range(f...  140 us
    reduce_scatter x1, waiting for transfers between devices, body(): owned = lax.psum_scatter(summed, 'head', scatter_dimension=2, tiled=True)  40.5 us
    ppermute x8, starting transfers between devices, from_behind(): lax.ppermute(value, axis, [(source, source + steps) for source in range(f...  24.5 us
    sub x8, other arithmetic, per_head(): weight_grads - row_terms  23.9 us
    dot_general x8, matrix products, per_head(): jnp.dot(score_grads, window_part[0], preferred_element_type=jnp.float32)  15.7 us
    unnamed x15, local copies, waits for them, and re-layouts  13.1 us
    dot_general x8, matrix products, per_head(): lax.dot_general(query_rows, window_part[0], inner_dims, preferred_element...  10.9 us
    dot_general x8, matrix products, per_head(): lax.dot_general(grad_rows, window_part[1], inner_dims, preferred_element_...  10.7 us
  transfers between devices with their start and end apart: 9, of which 8 were waited for; matrix products, arithmetic and copies ran while one was open for 3% of the time, Pallas kernels for 0%

commit v1 on v0

v1 whole, which is shorter than its diff:
```python
import functools
import math

import jax
import jax.numpy as jnp
import numpy as np
from jax import lax
from jax.experimental import pallas as pl
from jax.experimental.pallas import tpu as pltpu
from jax.sharding import PartitionSpec as P

HEAD = 128
BLOCK = 128
BEHIND = 512
SPAN = BLOCK + BEHIND
CHUNK = 256
OWN_HEADS = 4

rope_theta = 500000.0
rope_factor = 128.0
initial_context = 8192.0
ramp_low = 1.0
ramp_high = 32.0
attention_factor = 1.0 + 0.1 * math.log(rope_factor)
score_scale = 1.0 / math.sqrt(HEAD)
exponent_scale = score_scale / math.log(2.0)
EXCLUDED = -1e30

MESH = pl.DeviceIdType.MESH
NT = (((1,), (1,)), ((), ()))


def yarn_frequencies():
    halves = HEAD // 2
    powers = rope_theta ** (-2.0 * np.arange(halves) / HEAD)
    turns = initial_context * powers / (2.0 * np.pi)
    blend = np.clip((turns - ramp_low) / (ramp_high - ramp_low), 0.0, 1.0)
    return jnp.asarray(powers * ((1.0 - blend) / rope_factor + blend), jnp.float32)


def rope_tables(positions):
    frequency = yarn_frequencies()
    frequency = jnp.concatenate([frequency, frequency])
    signs = jnp.where(jnp.arange(HEAD) < HEAD // 2, -1.0, 1.0).astype(jnp.float32)
    angles = positions.astype(jnp.float32)[:, None] * frequency[None, :]
    return attention_factor * jnp.cos(angles), signs[None, :] * (attention_factor * jnp.sin(angles))


def dot(a, b):
    return jnp.dot(a, b, preferred_element_type=jnp.float32)


def kernel(
    outer_count, inner_count, groups,
    q_ref, g_ref, k_ref, v_ref, cos_ref, sin_ref,
    dq_ref, dk_ref, dv_ref,
    qb, gb, kraw, kv, tab, bias, qr, ps, dss, kt, acc, rin, ysend, yin, dqs,
    local_sem, own_sem, xs_sem, xr_sem, ys_sem, yr_sem, cs_sem, cr_sem,
    gcs_sem, gcr_sem, gys_sem, gyr_sem, dql_sem, dqs_sem, dqr_sem,
):
    outer, inner, head = lax.axis_index("outer"), lax.axis_index("inner"), lax.axis_index("head")
    blocks = outer_count * inner_count
    block = outer * inner_count + inner
    core = lax.rem(inner, 2)
    other = 1 - head

    def at(distance):
        target = lax.rem(block + distance + blocks, blocks)
        return (lax.div(target, inner_count), lax.rem(target, inner_count), head)

    partner = (outer, inner, other)
    sibling = (outer, inner + 1 - 2 * core, head)
    rows = BLOCK * groups
    mine = head * (OWN_HEADS * HEAD)
    theirs = other * (OWN_HEADS * HEAD)

    def columns(base, h):
        return pl.ds(pl.multiple_of(base + h * HEAD, HEAD), HEAD)

    def remote(src, dst, send, recv, device):
        return pltpu.make_async_remote_copy(
            src_ref=src, dst_ref=dst, send_sem=send, recv_sem=recv, device_id=device, device_id_type=MESH
        )

    def own_q(h):
        return pltpu.make_async_copy(q_ref.at[:, columns(mine, h)], qb.at[0, h], own_sem.at[0, h])

    def own_g(h):
        return pltpu.make_async_copy(g_ref.at[:, columns(mine, h)], gb.at[0, h], own_sem.at[1, h])

    def own_v(h):
        return pltpu.make_async_copy(v_ref.at[:, columns(mine, h)], kv.at[h, 4, 1], local_sem.at[h])

    def own_k():
        return pltpu.make_async_copy(
            k_ref.at[:, pl.ds(pl.multiple_of(mine, HEAD), OWN_HEADS * HEAD)], kraw, local_sem.at[OWN_HEADS]
        )

    def x_q(h):
        return remote(q_ref.at[:, columns(theirs, h)], qb.at[1, h], xs_sem.at[0, h], xr_sem.at[0, h], partner)

    def x_g(h):
        return remote(g_ref.at[:, columns(theirs, h)], gb.at[1, h], xs_sem.at[1, h], xr_sem.at[1, h], partner)

    def y_kv(h, i):
        return remote(kv.at[h, 4], kv.at[h, 2 - 2 * i], ys_sem.at[h, i], yr_sem.at[h, i], at(2 * i + 2))

    def c_kv(h, i):
        return remote(
            kv.at[h, 4 - 2 * core - 2 * i], kv.at[h, 3 - 2 * i], cs_sem.at[h, i], cr_sem.at[h, i], sibling
        )

    def c_grad(h, i):
        return remote(acc.at[h, 3 - 2 * i], rin.at[h, i], gcs_sem.at[h, i], gcr_sem.at[h, i], sibling)

    def y_grad(h, i):
        return remote(ysend.at[h, i], yin.at[h, i], gys_sem.at[h, i], gyr_sem.at[h, i], at(-2 * i - 2))

    def own_dq(h):
        return pltpu.make_async_copy(dqs.at[0, h], dq_ref.at[:, columns(mine, h)], dql_sem.at[h])

    def x_dq(h):
        return remote(dqs.at[1, h], dq_ref.at[:, columns(mine, h)], dqs_sem.at[h], dqr_sem.at[h], partner)

    def x_dq_arrival(h):
        return remote(dqs.at[1, h], dq_ref.at[:, columns(theirs, h)], dqs_sem.at[h], dqr_sem.at[h], partner)

    own_k().start()
    for h in range(OWN_HEADS):
        own_v(h).start()
    barrier = pltpu.get_barrier_semaphore()
    peers = (partner, sibling, at(2), at(4), at(-2), at(-4))
    for peer in peers:
        pl.semaphore_signal(barrier, inc=1, device_id=peer, device_id_type=MESH)
    for h in range(OWN_HEADS):
        own_q(h).start()
        own_g(h).start()

    cosines, sines = cos_ref[...], sin_ref[...]
    own_k().wait()
    for h in range(OWN_HEADS):
        raw = kraw[:, h * HEAD:(h + 1) * HEAD].astype(jnp.float32)
        kv[h, 4, 0] = (raw * cosines + pltpu.roll(raw, HEAD // 2, 1) * sines).astype(jnp.bfloat16)
    for h in range(OWN_HEADS):
        own_v(h).wait()

    pl.semaphore_wait(barrier, len(peers))
    for h in range(OWN_HEADS):
        for i in range(2):
            y_kv(h, i).start()
        x_q(h).start()
        x_g(h).start()

    low = lax.broadcasted_iota(jnp.int32, (8, HEAD), 0) < 4
    for table, ref in ((0, cos_ref), (1, sin_ref)):
        for pair in range(BLOCK // 2):
            first = jnp.broadcast_to(ref[2 * pair:2 * pair + 1, :], (8, HEAD))
            second = jnp.broadcast_to(ref[2 * pair + 1:2 * pair + 2, :], (8, HEAD))
            tab[table, 8 * pair:8 * pair + 8, :] = jnp.where(low, first, second)
    for part in (0, 1):
        row = lax.broadcasted_iota(jnp.int32, (SPAN - 64, CHUNK), 0)
        token = lax.broadcasted_iota(jnp.int32, (SPAN - 64, CHUNK), 1) // groups
        allowed = (row > token) & (row <= token + BEHIND) & (block * BLOCK - BEHIND + 64 * part + row >= 0)
        bias[part] = jnp.where(allowed, 0.0, EXCLUDED).astype(jnp.float32)
    for low_precision in (ps, dss):
        low_precision[SPAN - 64:, :CHUNK] = jnp.zeros((64, CHUNK), jnp.bfloat16)
        low_precision[:64, CHUNK:] = jnp.zeros((64, CHUNK), jnp.bfloat16)

    def stage(h):
        for i in range(2):
            y_kv(h, i).wait_recv()
        for i in range(2):
            c_kv(h, i).start()

    def unit(h, source):
        raw = qb[source, h].astype(jnp.float32)
        rotated = (raw * tab[0] + pltpu.roll(raw, HEAD // 2, 1) * tab[1]).astype(jnp.bfloat16)
        qr[...] = rotated
        keys = kv[h, :, 0].reshape(SPAN, HEAD)
        values = kv[h, :, 1].reshape(SPAN, HEAD)
        for part in (0, 1):
            here = slice(CHUNK * part, CHUNK * part + CHUNK)
            seen = slice(64 * part, 64 * part + SPAN - 64)
            scores = lax.dot_general(keys[seen], qr[here], NT, preferred_element_type=jnp.float32) + bias[part]
            top = jnp.max(scores, 0, keepdims=True)
            raised = jnp.exp2((scores - top) * exponent_scale)
            weights = raised * (1.0 / jnp.sum(raised, 0, keepdims=True))
            grads = lax.dot_general(values[seen], gb[source, h, here], NT, preferred_element_type=jnp.float32)
            delta = jnp.sum(weights * grads, 0, keepdims=True)
            ps[seen, here] = weights.astype(jnp.bfloat16)
            dss[seen, here] = (weights * (grads - delta)).astype(jnp.bfloat16)
        key_part = dot(dss[...], qr[...]).reshape(5, BLOCK, HEAD)
        value_part = dot(ps[...], gb[source, h]).reshape(5, BLOCK, HEAD)
        if source == 0:
            acc[h, :, 0] = key_part
            acc[h, :, 1] = value_part
        else:
            acc[h, :, 0] += key_part
            acc[h, :, 1] += value_part
        query_part = dot(kt[...], dss[...]).T
        query_part = query_part * score_scale
        dqs[source, h] = (query_part * tab[0] - pltpu.roll(query_part, HEAD // 2, 1) * tab[1]).astype(jnp.bfloat16)

    def combine(h):
        for i in range(2):
            c_grad(h, i).wait_recv()
            slot = 4 - 2 * core - 2 * i
            acc[h, slot] += rin[h, i]
        for i in range(2):
            ysend[h, i] = acc[h, 2 - 2 * i].astype(jnp.bfloat16)
            y_grad(h, i).start()

    stage(0)

    @pl.loop(0, OWN_HEADS)
    def _(h):
        for i in range(2):
            c_kv(h, i).wait_recv()
        kt[...] = kv[h, :, 0].reshape(SPAN, HEAD).T
        own_q(h).wait()
        own_g(h).wait()
        unit(h, 0)
        own_dq(h).start()

        @pl.when(h + 1 < OWN_HEADS)
        def _():
            stage(h + 1)

        @pl.when(h > 0)
        def _():
            combine(h - 1)

        x_q(h).wait_recv()
        x_g(h).wait_recv()
        unit(h, 1)
        for i in range(2):
            c_grad(h, i).start()
        x_dq(h).start()

    combine(OWN_HEADS - 1)
    for h in range(OWN_HEADS):
        for i in range(2):
            y_grad(h, i).wait_recv()
        total = acc[h, 4] + yin[h, 0].astype(jnp.float32) + yin[h, 1].astype(jnp.float32)
        key_total = total[0] * score_scale
        dk_ref[:, h * HEAD:(h + 1) * HEAD] = (
            key_total * cosines - pltpu.roll(key_total, HEAD // 2, 1) * sines
        ).astype(jnp.bfloat16)
        dv_ref[:, h * HEAD:(h + 1) * HEAD] = total[1].astype(jnp.bfloat16)

    for h in range(OWN_HEADS):
        x_q(h).wait_send()
        x_g(h).wait_send()
        own_dq(h).wait()
        x_dq(h).wait_send()
        x_dq_arrival(h).wait_recv()
        for i in range(2):
            y_kv(h, i).wait_send()
            c_kv(h, i).wait_send()
            c_grad(h, i).wait_send()
            y_grad(h, i).wait_send()


def body(outer_count, inner_count, queries, keys, values, grad_out, positions):
    tokens, groups, width = queries.shape
    rows = tokens * groups
    half = OWN_HEADS * HEAD
    cosines, sines = rope_tables(positions)
    low, high = jnp.bfloat16, jnp.float32
    semaphores = pltpu.SemaphoreType.DMA
    pairs = (OWN_HEADS, 2)
    anywhere = pl.BlockSpec(memory_space=pl.ANY)
    on_chip = pl.BlockSpec(memory_space=pltpu.VMEM)
    dq, dk, dv = pl.pallas_call(
        functools.partial(kernel, outer_count, inner_count, groups),
        out_shape=(
            jax.ShapeDtypeStruct((rows, width), low),
            jax.ShapeDtypeStruct((tokens, half), low),
            jax.ShapeDtypeStruct((tokens, half), low),
        ),
        in_specs=[anywhere] * 4 + [on_chip] * 2,
        out_specs=(anywhere, on_chip, on_chip),
        scratch_shapes=[
            pltpu.VMEM((2, OWN_HEADS, rows, HEAD), low),
            pltpu.VMEM((2, OWN_HEADS, rows, HEAD), low),
            pltpu.VMEM((tokens, half), low),
            pltpu.VMEM((OWN_HEADS, 5, 2, BLOCK, HEAD), low),
            pltpu.VMEM((2, rows, HEAD), high),
            pltpu.VMEM((2, SPAN - 64, CHUNK), high),
            pltpu.VMEM((rows, HEAD), low),
            pltpu.VMEM((SPAN, rows), low),
            pltpu.VMEM((SPAN, rows), low),
            pltpu.VMEM((HEAD, SPAN), low),
            pltpu.VMEM((OWN_HEADS, 5, 2, BLOCK, HEAD), high),
            pltpu.VMEM((OWN_HEADS, 2, 2, BLOCK, HEAD), high),
            pltpu.VMEM((OWN_HEADS, 2, 2, BLOCK, HEAD), low),
            pltpu.VMEM((OWN_HEADS, 2, 2, BLOCK, HEAD), low),
            pltpu.VMEM((2, OWN_HEADS, rows, HEAD), low),
            semaphores((OWN_HEADS + 1,)),
            semaphores((2, OWN_HEADS)),
            semaphores((2, OWN_HEADS)),
            semaphores((2, OWN_HEADS)),
            semaphores(pairs),
            semaphores(pairs),
            semaphores(pairs),
            semaphores(pairs),
            semaphores(pairs),
            semaphores(pairs),
            semaphores(pairs),
            semaphores(pairs),
            semaphores((OWN_HEADS,)),
            semaphores((OWN_HEADS,)),
            semaphores((OWN_HEADS,)),
        ],
        compiler_params=pltpu.CompilerParams(collective_id=0, has_side_effects=True, vmem_limit_bytes=48 * 2**20),
    )(
        queries.reshape(rows, width),
        grad_out.reshape(rows, width),
        keys,
        values,
        cosines,
        sines,
    )
    return dq.reshape(tokens, groups, width), dk, dv


def solution(mesh):
    placed = (
        P(("outer", "inner"), "head", None),
        P(("outer", "inner"), None),
        P(("outer", "inner"), None),
        P(("outer", "inner"), "head", None),
        P(("outer", "inner")),
    )
    return jax.shard_map(
        functools.partial(body, mesh.shape["outer"], mesh.shape["inner"]),
        mesh=mesh,
        in_specs=placed,
        out_specs=(
            P(("outer", "inner"), "head", None),
            P(("outer", "inner"), "head"),
            P(("outer", "inner"), "head"),
        ),
        check_vma=False,
    )
```

time: 357 us -> 76.6 us (0.21)
  waiting for transfers between devices: 181 us -> 0 us
  Pallas kernels: 0 us -> 66.5 us
  other arithmetic: 45.6 us -> 0.97 us
  matrix products: 43.4 us -> 0 us
  local copies, waits for them, and re-layouts: 46.1 us -> 8.16 us
  starting transfers between devices: 24.6 us -> 0 us
  between operations: 14.3 us -> 0.68 us
    ppermute x8 -> x0, waiting for transfers between devices: 140 us -> none  [from_behind(): lax.ppermute(value, axis, [(source, source + steps) for source in range(f...]
    pallas_call x0 -> x1, Pallas kernels: none -> 66.5 us  [body(): pl.pallas_call(functools.partial(kernel, outer_count, inner_count, groups...]
    dot_general x40 -> x0, matrix products: 43.4 us -> none  [the longest x8 15.7 us: per_head(): jnp.dot(score_grads, window_part[0], preferred_element_type=jnp.float32)]
    reduce_scatter x1 -> x0, waiting for transfers between devices: 40.5 us -> none  [body(): owned = lax.psum_scatter(summed, 'head', scatter_dimension=2, tiled=True)]
    ppermute x8 -> x0, starting transfers between devices: 24.5 us -> none  [from_behind(): lax.ppermute(value, axis, [(source, source + steps) for source in range(f...]
    sub x8 -> x0, other arithmetic: 23.9 us -> none  [per_head(): weight_grads - row_terms]
    dynamic_slice x24 -> x0, local copies, waits for them, and re-layouts: 9.99 us -> none  [body(): lax.map(per_head, (query_heads, grad_heads, window_heads))]
    transpose x1 -> x0, local copies, waits for them, and re-layouts: 7.87 us -> none  [body(): pair_grads.transpose(1, 2, 0, 3)]
  transfers between devices with their start and end apart: 9 -> 0, of which waited for: 8 -> 0; matrix products, arithmetic and copies ran while one was open for 3% -> 0% of each run, Pallas kernels for 0% -> 0%
where the time goes in v1:
time: 76.6 us; the launch traced here: 76.3 us
  Pallas kernels  66.5 us (87%)
  local copies, waits for them, and re-layouts  8.16 us (11%)
  other arithmetic  0.97 us (1%)
    pallas_call x1, Pallas kernels, body(): pl.pallas_call(functools.partial(kernel, outer_count, inner_count, groups...  66.5 us
    unnamed x18, local copies, waits for them, and re-layouts  5.28 us

profile of v1, /device:TPU:1, one launch (start us, length us, event | category | flops | bytes accessed | tf_op | source)
XLA Modules:
  0.0 76.3 jit_solution(2608997892297602744)
XLA Ops:
  0.6 0.7 convert_element_type.3
  1.3 0.0 copy-start.7
  1.3 0.6 copy-done.7
  1.9 0.3 fusion.1
  2.3 0.0 copy-start.6
  2.3 1.4 %reshape.22.q_ref = bf16[512,1024]{1,0:T(8,128)(2,1)S(1)} reshape(bf16[128,4,1024]{2,1,0:T(4,128)(2,1)} %param.6) | data formatting | bytes 2097152 | tf_op jit(solution)/shard_map/reshape | solution.py:317
  3.7 0.1 copy-done.6
  3.8 0.0 copy-start
  3.8 0.3 reshape.23.g_ref
  4.1 0.7 copy-done
  4.8 0.0 copy-start.1
  4.8 0.9 %copy-done.1 = bf16[128,1024]{1,0:T(8,128)(2,1)S(1)} copy-done((bf16[128,1024]{1,0:T(8,128)(2,1)S(1)}, bf16[128,1024]{1,0:T(8,128)(2,1)}, u32[]{:S(2)}) %copy-start.1) | copy-done | bytes 262168
  5.7 66.5 %shard_map.85 = (bf16[512,1024]{1,0:T(8,128)(2,1)S(1)}, bf16[128,512]{1,0:T(8,128)(2,1)S(1)}, bf16[128,512]{1,0:T(8,128)(2,1)S(1)}) custom-call(bf16[512,1024]{1,0:T(8,128)(2,1)S(1)} %reshape.22.q_ref, bf16[512,1024]{1,0:T(8,128)(2,1)S(1)} %reshape.23.g_ref, bf16[128,1024]{1,0:T(8,128)(2,1)S(1)} %copy-done, bf16[128,1024]{1,0:T(8,128)(2,1)S(1)} %copy-done.1, ...), custom_call_target="tpu_custom_call" | custom-call | tf_op jit(solution)/shard_map/pallas_call | solution.py:274
  72.2 0.0 copy-start.2
  72.2 0.6 copy-done.2
  72.8 0.0 copy-start.4
  72.8 0.7 copy-done.4
  73.5 0.0 copy-start.5
  73.5 1.2 %reshape.24 = bf16[128,4,1024]{2,1,0:T(4,128)(2,1)} reshape(bf16[512,1024]{1,0:T(8,128)(2,1)S(1)} %get-tuple-element.6) | data formatting | bytes 2097152 | tf_op jit(solution)/shard_map/reshape | solution.py:324
  74.7 0.0 copy-done.5
  74.7 0.0 copy-start.3
  74.7 0.7 copy.11
  75.3 0.3 copy-done.3
  75.6 0.7 copy.12
  (1 shorter events, 0.0 us)
Async XLA Ops:
  1.3 0.7 copy-start.7
  2.3 1.5 %copy-start.6 = (bf16[128,4,1024]{2,1,0:T(4,128)(2,1)S(1)}, bf16[128,4,1024]{2,1,0:T(4,128)(2,1)}, u32[]{:S(2)}) copy-start(bf16[128,4,1024]{2,1,0:T(4,128)(2,1)} %param.9) | copy-start | bytes 3145732
  3.8 0.9 %copy-start = (bf16[128,1024]{1,0:T(8,128)(2,1)S(1)}, bf16[128,1024]{1,0:T(8,128)(2,1)}, u32[]{:S(2)}) copy-start(bf16[128,1024]{1,0:T(8,128)(2,1)} %k_ref.1) | copy-start | bytes 786436
  4.8 0.9 %copy-start.1 = (bf16[128,1024]{1,0:T(8,128)(2,1)S(1)}, bf16[128,1024]{1,0:T(8,128)(2,1)}, u32[]{:S(2)}) copy-start(bf16[128,1024]{1,0:T(8,128)(2,1)} %v_ref.1) | copy-start | bytes 786436
  72.2 0.6 copy-start.2
  72.8 0.7 copy-start.4
  73.5 1.2 %copy-start.5 = (bf16[128,512]{1,0:T(8,128)(2,1)S(1)}, bf16[128,512]{1,0:T(8,128)(2,1)}, u32[]{:S(2)}) copy-start(bf16[128,512]{1,0:T(8,128)(2,1)} %copy-done.4) | copy-start | bytes 393220
  74.7 1.0 %copy-start.3 = (bf16[128,512]{1,0:T(8,128)(2,1)S(1)}, bf16[128,512]{1,0:T(8,128)(2,1)}, u32[]{:S(2)}) copy-start(bf16[128,512]{1,0:T(8,128)(2,1)} %copy-done.2) | copy-start | bytes 393220

commit v2 on v1

v2 whole, which is shorter than its diff:
```python
import functools
import math

import jax
import jax.numpy as jnp
import numpy as np
from jax import lax
from jax.experimental import pallas as pl
from jax.experimental.pallas import tpu as pltpu
from jax.sharding import PartitionSpec as P

HEAD = 128
BLOCK = 128
BEHIND = 512
SPAN = BLOCK + BEHIND
CHUNK = 256
OWN_HEADS = 4
SHARED = 1
PLACES = OWN_HEADS + SHARED

rope_theta = 500000.0
rope_factor = 128.0
initial_context = 8192.0
ramp_low = 1.0
ramp_high = 32.0
attention_factor = 1.0 + 0.1 * math.log(rope_factor)
score_scale = 1.0 / math.sqrt(HEAD)
exponent_scale = score_scale / math.log(2.0)
EXCLUDED = -1e30

MESH = pl.DeviceIdType.MESH
NT = (((1,), (1,)), ((), ()))


def yarn_frequencies():
    halves = HEAD // 2
    powers = rope_theta ** (-2.0 * np.arange(halves) / HEAD)
    turns = initial_context * powers / (2.0 * np.pi)
    blend = np.clip((turns - ramp_low) / (ramp_high - ramp_low), 0.0, 1.0)
    return jnp.asarray(powers * ((1.0 - blend) / rope_factor + blend), jnp.float32)


def rope_tables(positions):
    frequency = yarn_frequencies()
    frequency = jnp.concatenate([frequency, frequency])
    signs = jnp.where(jnp.arange(HEAD) < HEAD // 2, -1.0, 1.0).astype(jnp.float32)
    angles = positions.astype(jnp.float32)[:, None] * frequency[None, :]
    return attention_factor * jnp.cos(angles), signs[None, :] * (attention_factor * jnp.sin(angles))


def dot(a, b):
    return jnp.dot(a, b, preferred_element_type=jnp.float32)


def kernel(
    outer_count, inner_count, groups,
    q_ref, g_ref, k_ref, v_ref, cos_ref, sin_ref,
    dq_ref, dk_ref, dv_ref,
    qb, gb, qr, kraw, kv, tab, bias, ps, dss, kt, acc, rin, ysend, yin, dqs, fsend, fin, done,
    k_sem, v_sem, q_sem, g_sem, xs_sem, xr_sem, ys_sem, yr_sem, cs_sem, cr_sem,
    gcs_sem, gcr_sem, gys_sem, gyr_sem, dql_sem, dqs_sem, dqr_sem, fs_sem, fr_sem, os_sem, or_sem,
):
    outer, inner, head = lax.axis_index("outer"), lax.axis_index("inner"), lax.axis_index("head")
    blocks = outer_count * inner_count
    half_outer = outer_count // 2
    block = outer * inner_count + inner
    core = lax.rem(inner, 2)
    flip = lax.div(outer, half_outer)
    owner = lax.rem(head + flip, 2)

    def at(distance):
        target = lax.rem(block + distance + blocks, blocks)
        target_outer = lax.div(target, inner_count)
        target_head = lax.rem(owner + lax.div(target_outer, half_outer), 2)
        return (target_outer, lax.rem(target, inner_count), target_head)

    partner = (outer, inner, 1 - head)
    sibling = (outer, inner + 1 - 2 * core, head)
    ahead, back = at(2), at(-2)
    mine = owner * (OWN_HEADS * HEAD)
    theirs = (1 - owner) * (OWN_HEADS * HEAD)

    def columns(start):
        return pl.ds(pl.multiple_of(start, HEAD), HEAD)

    def column_of(p):
        if isinstance(p, int):
            return theirs + p * HEAD if p < SHARED else mine + (p - SHARED) * HEAD
        kept = lax.min(lax.div(p, SHARED), 1) if SHARED else 1
        return theirs + p * HEAD + kept * (mine - theirs - SHARED * HEAD)

    def local(src, dst, sem):
        return pltpu.make_async_copy(src, dst, sem)

    def remote(src, dst, send, recv, device):
        return pltpu.make_async_remote_copy(
            src_ref=src, dst_ref=dst, send_sem=send, recv_sem=recv, device_id=device, device_id_type=MESH
        )

    def own_k(p):
        return local(k_ref.at[:, columns(column_of(p))], kraw.at[p], k_sem.at[p])

    def own_v(p):
        return local(v_ref.at[:, columns(column_of(p))], kv.at[p, 4, 1], v_sem.at[p])

    def own_q(p):
        return local(q_ref.at[:, columns(column_of(p))], qb.at[p], q_sem.at[p])

    def own_g(p):
        return local(g_ref.at[:, columns(column_of(p))], gb.at[p], g_sem.at[p])

    def x_q(p):
        n = p - 2 * SHARED
        return remote(
            q_ref.at[:, columns(theirs + (p - SHARED) * HEAD)], qb.at[PLACES + n], xs_sem.at[0, n], xr_sem.at[0, n], partner
        )

    def x_g(p):
        n = p - 2 * SHARED
        return remote(
            g_ref.at[:, columns(theirs + (p - SHARED) * HEAD)], gb.at[PLACES + n], xs_sem.at[1, n], xr_sem.at[1, n], partner
        )

    def y_kv(p, i):
        return remote(kv.at[p, 4 - 2 * i], kv.at[p, 2 - 2 * i], ys_sem.at[p, i], yr_sem.at[p, i], ahead)

    def c_kv(p, i):
        return remote(
            kv.at[p, 4 - 2 * core - 2 * i], kv.at[p, 3 - 2 * i], cs_sem.at[p, i], cr_sem.at[p, i], sibling
        )

    def c_grad(p, i):
        return remote(acc.at[p, 3 - 2 * i], rin.at[p, i], gcs_sem.at[p, i], gcr_sem.at[p, i], sibling)

    def y_grad(p, i):
        return remote(ysend.at[p, i], yin.at[p, i], gys_sem.at[p, i], gyr_sem.at[p, i], back)

    def own_dq(p):
        return local(dqs.at[p], dq_ref.at[:, columns(column_of(p))], dql_sem.at[p])

    def x_dq(p, start):
        n = p - 2 * SHARED
        return remote(
            dqs.at[PLACES + n], dq_ref.at[:, columns(start + (p - SHARED) * HEAD)], dqs_sem.at[n], dqr_sem.at[n], partner
        )

    def x_shared(i):
        return remote(fsend.at[i], fin.at[i], fs_sem.at[i], fr_sem.at[i], partner)

    def results(p):
        here = pl.ds((p - SHARED) * HEAD, HEAD)
        return ((done.at[p, 0], dk_ref.at[:, here]), (done.at[p, 1], dv_ref.at[:, here]))

    def own_out(p, i):
        src, dst = results(p)[i]
        return local(src, dst, os_sem.at[p, i])

    def x_out(p, i):
        src, dst = results(p)[i]
        return remote(src, dst, os_sem.at[p, i], or_sem.at[p, i], partner)

    for p in range(PLACES):
        own_k(p).start()
        own_v(p).start()
    barrier = pltpu.get_barrier_semaphore()
    peers = (partner, sibling, ahead, back)
    for peer in peers:
        pl.semaphore_signal(barrier, inc=1, device_id=peer, device_id_type=MESH)
    for p in range(PLACES):
        own_q(p).start()
        own_g(p).start()

    cosines, sines = cos_ref[...], sin_ref[...]
    for p in range(PLACES):
        own_k(p).wait()
        raw = kraw[p].astype(jnp.float32)
        kv[p, 4, 0] = (raw * cosines + pltpu.roll(raw, HEAD // 2, 1) * sines).astype(jnp.bfloat16)
    for p in range(PLACES):
        own_v(p).wait()

    pl.semaphore_wait(barrier, len(peers))
    for p in range(2):
        y_kv(p, 0).start()
    for p in range(2 * SHARED, PLACES):
        x_q(p).start()
        x_g(p).start()

    def stage_a(p):
        y_kv(p, 0).wait_recv()
        y_kv(p, 1).start()
        if isinstance(p, int):
            y_kv(p + 2, 0).start()
        else:
            @pl.when(p + 2 < PLACES)
            def _():
                y_kv(p + 2, 0).start()
        c_kv(p, 0).start()

    def stage_b(p):
        y_kv(p, 1).wait_recv()
        c_kv(p, 1).start()

    low = lax.broadcasted_iota(jnp.int32, (8, HEAD), 0) < 4
    for table, ref in ((0, cos_ref), (1, sin_ref)):
        for pair in range(BLOCK // 2):
            first = jnp.broadcast_to(ref[2 * pair:2 * pair + 1, :], (8, HEAD))
            second = jnp.broadcast_to(ref[2 * pair + 1:2 * pair + 2, :], (8, HEAD))
            tab[table, 8 * pair:8 * pair + 8, :] = jnp.where(low, first, second)

    stage_a(0)
    for part in (0, 1):
        row = lax.broadcasted_iota(jnp.int32, (SPAN - 64, CHUNK), 0)
        token = lax.broadcasted_iota(jnp.int32, (SPAN - 64, CHUNK), 1) // groups
        allowed = (row > token) & (row <= token + BEHIND) & (block * BLOCK - BEHIND + 64 * part + row >= 0)
        bias[part] = jnp.where(allowed, 0.0, EXCLUDED).astype(jnp.float32)
    for low_precision in (ps, dss):
        low_precision[SPAN - 64:, :CHUNK] = jnp.zeros((64, CHUNK), jnp.bfloat16)
        low_precision[:64, CHUNK:] = jnp.zeros((64, CHUNK), jnp.bfloat16)
    stage_a(1)

    def rotate_queries(n):
        raw = qb[n].astype(jnp.float32)
        qr[n] = (raw * tab[0] + pltpu.roll(raw, HEAD // 2, 1) * tab[1]).astype(jnp.bfloat16)

    @pl.loop(0, PLACES)
    def _(p):
        own_q(p).wait()
        own_g(p).wait()
        rotate_queries(p)

    stage_b(0)

    def unit(p, n, first):
        keys = kv[p, :, 0].reshape(SPAN, HEAD)
        values = kv[p, :, 1].reshape(SPAN, HEAD)
        for part in (0, 1):
            here = slice(CHUNK * part, CHUNK * part + CHUNK)
            seen = slice(64 * part, 64 * part + SPAN - 64)
            scores = lax.dot_general(keys[seen], qr[n, here], NT, preferred_element_type=jnp.float32) + bias[part]
            top = jnp.max(scores, 0, keepdims=True)
            raised = jnp.exp2((scores - top) * exponent_scale)
            weights = raised * (1.0 / jnp.sum(raised, 0, keepdims=True))
            grads = lax.dot_general(values[seen], gb[n, here], NT, preferred_element_type=jnp.float32)
            delta = jnp.sum(weights * grads, 0, keepdims=True)
            ps[seen, here] = weights.astype(jnp.bfloat16)
            dss[seen, here] = (weights * (grads - delta)).astype(jnp.bfloat16)
        key_part = dot(dss[...], qr[n]).reshape(5, BLOCK, HEAD)
        value_part = dot(ps[...], gb[n]).reshape(5, BLOCK, HEAD)
        if first:
            acc[p, :, 0] = key_part
            acc[p, :, 1] = value_part
        else:
            acc[p, :, 0] += key_part
            acc[p, :, 1] += value_part
        query_part = dot(kt[...], dss[...]).T
        query_part = query_part * score_scale
        dqs[n] = (query_part * tab[0] - pltpu.roll(query_part, HEAD // 2, 1) * tab[1]).astype(jnp.bfloat16)

    def combine_a(p):
        for i in range(2):
            c_grad(p, i).wait_recv()
            acc[p, 4 - 2 * core - 2 * i] += rin[p, i]
        ysend[p, 1] = acc[p, 0].astype(jnp.bfloat16)
        y_grad(p, 1).start()

    def combine_b(p):
        y_grad(p, 1).wait_recv()
        ysend[p, 0] = (acc[p, 2] + yin[p, 1].astype(jnp.float32)).astype(jnp.bfloat16)
        y_grad(p, 0).start()

    def total_of(p):
        y_grad(p, 0).wait_recv()
        return acc[p, 4] + yin[p, 0].astype(jnp.float32)

    def send_shared():
        for i in range(SHARED):
            fsend[i] = total_of(flip * SHARED + i).astype(jnp.bfloat16)
            x_shared(i).start()

    def finish(p, total):
        key_total = total[0] * score_scale
        done[p, 0] = (key_total * cosines - pltpu.roll(key_total, HEAD // 2, 1) * sines).astype(jnp.bfloat16)
        done[p, 1] = total[1].astype(jnp.bfloat16)

    def finish_swapped(p):
        finish(p, total_of(p))

        @pl.when(flip == 0)
        def _():
            for i in range(2):
                own_out(p, i).start()

        @pl.when(flip == 1)
        def _():
            for i in range(2):
                x_out(p, i).start()

    def position(p, swapped):
        for i in range(2):
            c_kv(p, i).wait_recv()
        kt[...] = kv[p, :, 0].reshape(SPAN, HEAD).T

        @pl.when(p + 2 < PLACES)
        def _():
            stage_a(p + 2)

        unit(p, p, True)
        own_dq(p).start()
        if not swapped:
            for i in range(2):
                c_grad(p, i).start()

        @pl.when(p + 1 < PLACES)
        def _():
            stage_b(p + 1)

        @pl.when(p > 0)
        def _():
            combine_a(p - 1)

        @pl.when(p > 1)
        def _():
            combine_b(p - 2)

        if swapped:
            if early_shared:
                @pl.when(p == PLACES - 1)
                def _():
                    send_shared()
            n = PLACES + p - 2 * SHARED
            x_q(p).wait_recv()
            x_g(p).wait_recv()
            rotate_queries(n)
            unit(p, n, False)
            for i in range(2):
                c_grad(p, i).start()
            x_dq(p, mine).start()

    early_shared = 2 * SHARED + 2 < PLACES
    if SHARED:
        @pl.loop(0, 2 * SHARED)
        def _(p):
            position(p, False)

    @pl.loop(2 * SHARED, PLACES)
    def _(p):
        position(p, True)

    combine_a(PLACES - 1)
    combine_b(PLACES - 2)
    if not early_shared:
        send_shared()
    for p in range(2 * SHARED, PLACES - 2):
        finish_swapped(p)
    combine_b(PLACES - 1)
    for p in range(max(2 * SHARED, PLACES - 2), PLACES - 1):
        finish_swapped(p)
    for i in range(SHARED):
        p = (1 - flip) * SHARED + i
        total = total_of(p)
        x_shared(i).wait_recv()
        finish(SHARED + i, total + fin[i].astype(jnp.float32))
        for o in range(2):
            own_out(SHARED + i, o).start()
    finish_swapped(PLACES - 1)

    for p in range(PLACES):
        own_dq(p).wait()
        for i in range(2):
            y_kv(p, i).wait_send()
            c_kv(p, i).wait_send()
            c_grad(p, i).wait_send()
            y_grad(p, i).wait_send()
    for i in range(SHARED):
        x_shared(i).wait_send()
        for o in range(2):
            own_out(SHARED + i, o).wait()
    for p in range(2 * SHARED, PLACES):
        x_q(p).wait_send()
        x_g(p).wait_send()
        x_dq(p, mine).wait_send()
        x_dq(p, theirs).wait_recv()

    @pl.when(flip == 0)
    def _():
        for p in range(2 * SHARED, PLACES):
            for i in range(2):
                own_out(p, i).wait()

    @pl.when(flip == 1)
    def _():
        for p in range(2 * SHARED, PLACES):
            for i in range(2):
                x_out(p, i).wait_send()
                x_out(p, i).wait_recv()


def body(outer_count, inner_count, queries, keys, values, grad_out, positions):
    tokens, groups, width = queries.shape
    rows = tokens * groups
    half = OWN_HEADS * HEAD
    cosines, sines = rope_tables(positions)
    low, high = jnp.bfloat16, jnp.float32
    semaphores = pltpu.SemaphoreType.DMA
    swapped = OWN_HEADS - SHARED
    pairs = (PLACES, 2)
    anywhere = pl.BlockSpec(memory_space=pl.ANY)
    off_chip = pl.BlockSpec(memory_space=pltpu.HBM)
    on_chip = pl.BlockSpec(memory_space=pltpu.VMEM)
    dq, dk, dv = pl.pallas_call(
        functools.partial(kernel, outer_count, inner_count, groups),
        out_shape=(
            jax.ShapeDtypeStruct((rows, width), low),
            jax.ShapeDtypeStruct((tokens, half), low),
            jax.ShapeDtypeStruct((tokens, half), low),
        ),
        in_specs=[anywhere] * 2 + [off_chip] * 2 + [on_chip] * 2,
        out_specs=(anywhere, off_chip, off_chip),
        scratch_shapes=[
            pltpu.VMEM((2 * OWN_HEADS, rows, HEAD), low),
            pltpu.VMEM((2 * OWN_HEADS, rows, HEAD), low),
            pltpu.VMEM((2 * OWN_HEADS, rows, HEAD), low),
            pltpu.VMEM((PLACES, tokens, HEAD), low),
            pltpu.VMEM((PLACES, 5, 2, BLOCK, HEAD), low),
            pltpu.VMEM((2, rows, HEAD), high),
            pltpu.VMEM((2, SPAN - 64, CHUNK), high),
            pltpu.VMEM((SPAN, rows), low),
            pltpu.VMEM((SPAN, rows), low),
            pltpu.VMEM((HEAD, SPAN), low),
            pltpu.VMEM((PLACES, 5, 2, BLOCK, HEAD), high),
            pltpu.VMEM((PLACES, 2, 2, BLOCK, HEAD), high),
            pltpu.VMEM((PLACES, 2, 2, BLOCK, HEAD), low),
            pltpu.VMEM((PLACES, 2, 2, BLOCK, HEAD), low),
            pltpu.VMEM((2 * OWN_HEADS, rows, HEAD), low),
            pltpu.VMEM((max(SHARED, 1), 2, BLOCK, HEAD), low),
            pltpu.VMEM((max(SHARED, 1), 2, BLOCK, HEAD), low),
            pltpu.VMEM((PLACES, 2, BLOCK, HEAD), low),
            semaphores((PLACES,)),
            semaphores((PLACES,)),
            semaphores((PLACES,)),
            semaphores((PLACES,)),
            semaphores((2, swapped)),
            semaphores((2, swapped)),
            semaphores(pairs),
            semaphores(pairs),
            semaphores(pairs),
            semaphores(pairs),
            semaphores(pairs),
            semaphores(pairs),
            semaphores(pairs),
            semaphores(pairs),
            semaphores((PLACES,)),
            semaphores((swapped,)),
            semaphores((swapped,)),
            semaphores((max(SHARED, 1),)),
            semaphores((max(SHARED, 1),)),
            semaphores(pairs),
            semaphores(pairs),
        ],
        compiler_params=pltpu.CompilerParams(collective_id=0, has_side_effects=True, vmem_limit_bytes=48 * 2**20),
    )(
        queries.reshape(rows, width),
        grad_out.reshape(rows, width),
        keys,
        values,
        cosines,
        sines,
    )
    return dq.reshape(tokens, groups, width), dk, dv


def solution(mesh):
    placed = (
        P(("outer", "inner"), "head", None),
        P(("outer", "inner"), None),
        P(("outer", "inner"), None),
        P(("outer", "inner"), "head", None),
        P(("outer", "inner")),
    )
    return jax.shard_map(
        functools.partial(body, mesh.shape["outer"], mesh.shape["inner"]),
        mesh=mesh,
        in_specs=placed,
        out_specs=(
            P(("outer", "inner"), "head", None),
            P(("outer", "inner"), "head"),
            P(("outer", "inner"), "head"),
        ),
        check_vma=False,
    )
```

time: 76.6 us -> 65.7 us (0.86)
  the two profiles are of different devices: /device:TPU:1 before, /device:TPU:4 now
where the time goes in v2:
time: 65.7 us; the launch traced here: 65.5 us
  Pallas kernels  55.6 us (85%)
  local copies, waits for them, and re-layouts  8.16 us (12%)
  other arithmetic  0.97 us (1%)
  between operations  0.68 us (1%)
    pallas_call x1, Pallas kernels, body(): pl.pallas_call(functools.partial(kernel, outer_count, inner_count, groups...  55.6 us
    unnamed x18, local copies, waits for them, and re-layouts  5.28 us
    reshape x1, local copies, waits for them, and re-layouts, body(): queries.reshape(rows, width)  1.43 us

profile of v2, /device:TPU:4, one launch (start us, length us, event | category | flops | bytes accessed | tf_op | source)
XLA Modules:
  0.0 65.5 jit_solution(8923110311113031923)
XLA Ops:
  0.6 0.7 %convert_element_type.3 = f32[128]{0:T(128)S(1)} convert(s32[128]{0:T(128)} %param.10) | non-fusion elementwise | flops 128 | bytes 1024 | tf_op jit(solution)/shard_map/convert_element_type | solution.py:47
  1.3 0.0 copy-start.7
  1.3 0.6 copy-done.7
  1.9 0.3 fusion.1
  2.3 0.0 copy-start.6
  2.3 1.4 %reshape.22.q_ref = bf16[512,1024]{1,0:T(8,128)(2,1)S(1)} reshape(bf16[128,4,1024]{2,1,0:T(4,128)(2,1)} %param.6) | data formatting | bytes 2097152 | tf_op jit(solution)/shard_map/reshape | solution.py:462
  3.7 0.1 copy-done.6
  3.8 0.0 copy-start
  3.8 0.3 reshape.23.g_ref
  4.1 0.7 %copy-done = bf16[128,1024]{1,0:T(8,128)(2,1)S(1)} copy-done((bf16[128,1024]{1,0:T(8,128)(2,1)S(1)}, bf16[128,1024]{1,0:T(8,128)(2,1)}, u32[]{:S(2)}) %copy-start) | copy-done | bytes 262168
  4.8 0.0 copy-start.1
  4.8 0.9 %copy-done.1 = bf16[128,1024]{1,0:T(8,128)(2,1)S(1)} copy-done((bf16[128,1024]{1,0:T(8,128)(2,1)S(1)}, bf16[128,1024]{1,0:T(8,128)(2,1)}, u32[]{:S(2)}) %copy-start.1) | copy-done | bytes 262168
  5.7 55.6 %shard_map.85 = (bf16[512,1024]{1,0:T(8,128)(2,1)S(1)}, bf16[128,512]{1,0:T(8,128)(2,1)S(1)}, bf16[128,512]{1,0:T(8,128)(2,1)S(1)}) custom-call(bf16[512,1024]{1,0:T(8,128)(2,1)S(1)} %reshape.22.q_ref, bf16[512,1024]{1,0:T(8,128)(2,1)S(1)} %reshape.23.g_ref, bf16[128,1024]{1,0:T(8,128)(2,1)S(1)} %copy-done, bf16[128,1024]{1,0:T(8,128)(2,1)S(1)} %copy-done.1, ...), custom_call_target="tpu_custom_call" | custom-call | tf_op jit(solution)/shard_map/pallas_call | solution.py:410
  61.4 0.0 copy-start.2
  61.4 0.6 copy-done.2
  62.0 0.0 copy-start.4
  62.0 0.7 copy-done.4
  62.7 0.0 copy-start.5
  62.7 1.2 %reshape.24 = bf16[128,4,1024]{2,1,0:T(4,128)(2,1)} reshape(bf16[512,1024]{1,0:T(8,128)(2,1)S(1)} %get-tuple-element.6) | data formatting | bytes 2097152 | tf_op jit(solution)/shard_map/reshape | solution.py:469
  63.9 0.0 copy-done.5
  63.9 0.0 copy-start.3
  63.9 0.7 %copy.11 = bf16[128,512]{1,0:T(8,128)(2,1)} copy(bf16[128,512]{1,0:T(8,128)(2,1)S(1)} %copy-done.5) | data formatting | bytes 262144
  64.5 0.3 copy-done.3
  64.8 0.7 %copy.12 = bf16[128,512]{1,0:T(8,128)(2,1)} copy(bf16[128,512]{1,0:T(8,128)(2,1)S(1)} %copy-done.3) | data formatting | bytes 262144
  (1 shorter events, 0.0 us)
Async XLA Ops:
  1.3 0.7 %copy-start.7 = (f32[128]{0:T(128)S(1)}, f32[128]{0:T(128)}, u32[]{:S(2)}) copy-start(f32[128]{0:T(128)} %constant.16) | copy-start | bytes 1540
  2.3 1.5 %copy-start.6 = (bf16[128,4,1024]{2,1,0:T(4,128)(2,1)S(1)}, bf16[128,4,1024]{2,1,0:T(4,128)(2,1)}, u32[]{:S(2)}) copy-start(bf16[128,4,1024]{2,1,0:T(4,128)(2,1)} %param.9) | copy-start | bytes 3145732
  3.8 0.9 %copy-start = (bf16[128,1024]{1,0:T(8,128)(2,1)S(1)}, bf16[128,1024]{1,0:T(8,128)(2,1)}, u32[]{:S(2)}) copy-start(bf16[128,1024]{1,0:T(8,128)(2,1)} %k_ref.1) | copy-start | bytes 786436
  4.8 0.9 %copy-start.1 = (bf16[128,1024]{1,0:T(8,128)(2,1)S(1)}, bf16[128,1024]{1,0:T(8,128)(2,1)}, u32[]{:S(2)}) copy-start(bf16[128,1024]{1,0:T(8,128)(2,1)} %v_ref.1) | copy-start | bytes 786436
  61.4 0.6 copy-start.2
  62.0 0.7 %copy-start.4 = (bf16[128,512]{1,0:T(8,128)(2,1)}, bf16[128,512]{1,0:T(8,128)(2,1)S(1)}, u32[]{:S(2)}) copy-start(bf16[128,512]{1,0:T(8,128)(2,1)S(1)} %get-tuple-element.15) | copy-start | bytes 393220
  62.7 1.2 %copy-start.5 = (bf16[128,512]{1,0:T(8,128)(2,1)S(1)}, bf16[128,512]{1,0:T(8,128)(2,1)}, u32[]{:S(2)}) copy-start(bf16[128,512]{1,0:T(8,128)(2,1)} %copy-done.4) | copy-start | bytes 393220
  63.9 1.0 %copy-start.3 = (bf16[128,512]{1,0:T(8,128)(2,1)S(1)}, bf16[128,512]{1,0:T(8,128)(2,1)}, u32[]{:S(2)}) copy-start(bf16[128,512]{1,0:T(8,128)(2,1)} %copy-done.2) | copy-start | bytes 393220

commit v3 on v2

v3 whole, which is shorter than its diff:
```python
import functools
import math

import jax
import jax.numpy as jnp
import numpy as np
from jax import lax
from jax.experimental import pallas as pl
from jax.experimental.pallas import tpu as pltpu
from jax.sharding import PartitionSpec as P

HEAD = 128
BLOCK = 128
BEHIND = 512
SPAN = BLOCK + BEHIND
CHUNK = 256
OWN_HEADS = 4
PLACES = OWN_HEADS
SETTLE = 4

rope_theta = 500000.0
rope_factor = 128.0
initial_context = 8192.0
ramp_low = 1.0
ramp_high = 32.0
attention_factor = 1.0 + 0.1 * math.log(rope_factor)
score_scale = 1.0 / math.sqrt(HEAD)
exponent_scale = score_scale / math.log(2.0)
EXCLUDED = -1e30

MESH = pl.DeviceIdType.MESH
NT = (((1,), (1,)), ((), ()))


def yarn_frequencies():
    halves = HEAD // 2
    powers = rope_theta ** (-2.0 * np.arange(halves) / HEAD)
    turns = initial_context * powers / (2.0 * np.pi)
    blend = np.clip((turns - ramp_low) / (ramp_high - ramp_low), 0.0, 1.0)
    return np.asarray(powers * ((1.0 - blend) / rope_factor + blend), np.float32)


TURN_HIGH = 6.28125
TURN_MIDDLE = math.floor((2.0 * math.pi - TURN_HIGH) * 2.0**20) / 2.0**20
TURN_LOW = 2.0 * math.pi - TURN_HIGH - TURN_MIDDLE


def rope_tables(positions):
    lane = lax.broadcasted_iota(jnp.int32, (8, HEAD), 1)
    frequency = jnp.zeros((8, HEAD), jnp.float32)
    for index, value in enumerate(yarn_frequencies()):
        frequency = jnp.where(lax.rem(lane, HEAD // 2) == index, float(value), frequency)
    times = jnp.broadcast_to(positions.astype(jnp.float32), (BLOCK, HEAD)).T
    angles = times * frequency[0:1]
    turns = jnp.floor(angles * (0.5 / math.pi) + 0.5)
    rest = ((angles - turns * TURN_HIGH) - turns * TURN_MIDDLE) - turns * TURN_LOW
    signed = jnp.where(lane[0:1] < HEAD // 2, -attention_factor, attention_factor)
    return attention_factor * jnp.cos(rest), signed * jnp.sin(rest)


def dot(a, b):
    return jnp.dot(a, b, preferred_element_type=jnp.float32)


def kernel(
    outer_count, inner_count, groups,
    q_ref, g_ref, k_ref, v_ref, pos_ref,
    dq_ref, dkv_ref,
    qb, gb, qr, gr, kraw, kv, pos, small, tab, bias, ps, dss, kt, acc, rin, ysend, yin, dqs, done,
    pos_sem, k_sem, v_sem, q_sem, g_sem, xs_sem, xr_sem, ys_sem, yr_sem, cs_sem, cr_sem,
    gcs_sem, gcr_sem, gys_sem, gyr_sem, dql_sem, dqs_sem, dqr_sem, os_sem, or_sem,
):
    outer, inner, head = lax.axis_index("outer"), lax.axis_index("inner"), lax.axis_index("head")
    blocks = outer_count * inner_count
    half_outer = outer_count // 2
    block = outer * inner_count + inner
    core = lax.rem(inner, 2)
    later = lax.div(outer, half_outer)
    flip = 1 - later
    owner = lax.rem(head + flip, 2)
    first, last = block < 2, block >= blocks - 2
    has_back, has_ahead = block >= 2, block < blocks - 2

    def at(distance):
        target = lax.rem(block + distance + blocks, blocks)
        target_outer = lax.div(target, inner_count)
        target_head = lax.rem(owner + 1 - lax.div(target_outer, half_outer), 2)
        return (target_outer, lax.rem(target, inner_count), target_head)

    partner = (outer, inner, 1 - head)
    sibling = (outer, inner + 1 - 2 * core, head)
    ahead, back = at(2), at(-2)
    rows = BLOCK * groups
    mine = owner * (OWN_HEADS * HEAD)
    theirs = (1 - owner) * (OWN_HEADS * HEAD)

    def columns(start):
        return pl.ds(pl.multiple_of(start, HEAD), HEAD)

    def column_of(p):
        return mine + p * HEAD

    def local(src, dst, sem):
        return pltpu.make_async_copy(src, dst, sem)

    def remote(src, dst, send, recv, device):
        return pltpu.make_async_remote_copy(
            src_ref=src, dst_ref=dst, send_sem=send, recv_sem=recv, device_id=device, device_id_type=MESH
        )

    def own_k(p):
        return local(k_ref.at[:, columns(column_of(p))], kraw.at[p], k_sem.at[p])

    def own_v(p):
        return local(v_ref.at[:, columns(column_of(p))], kv.at[p, 4, 1], v_sem.at[p])

    def own_q(p):
        return local(q_ref.at[:, :, columns(column_of(p))], qb.at[p], q_sem.at[p])

    def own_g(p):
        return local(g_ref.at[:, :, columns(column_of(p))], gb.at[p], g_sem.at[p])

    def x_q(p):
        return remote(q_ref.at[:, :, columns(theirs + p * HEAD)], qb.at[PLACES + p], xs_sem.at[0, p], xr_sem.at[0, p], partner)

    def x_g(p):
        return remote(g_ref.at[:, :, columns(theirs + p * HEAD)], gb.at[PLACES + p], xs_sem.at[1, p], xr_sem.at[1, p], partner)

    def y_kv(p, i, kind):
        n = 2 * i + kind
        return remote(kv.at[p, 4 - 2 * i, kind], kv.at[p, 2 - 2 * i, kind], ys_sem.at[p, n], yr_sem.at[p, n], ahead)

    def c_kv(p, i, kind):
        n = 2 * i + kind
        src = kv.at[p, 4 - 2 * core - 2 * i, kind]
        return remote(src, kv.at[p, 3 - 2 * i, kind], cs_sem.at[p, n], cr_sem.at[p, n], sibling)

    def c_grad(p, i, kind):
        n = 2 * i + kind
        return remote(acc.at[p, 3 - 2 * i, kind], rin.at[p, i, kind], gcs_sem.at[p, n], gcr_sem.at[p, n], sibling)

    def y_grad(p, i, kind):
        n = 2 * i + kind
        return remote(ysend.at[p, i, kind], yin.at[p, i, kind], gys_sem.at[p, n], gyr_sem.at[p, n], back)

    def own_dq(p):
        return local(dqs.at[p], dq_ref.at[:, :, columns(column_of(p))], dql_sem.at[p])

    def x_dq(p, start):
        return remote(
            dqs.at[PLACES + p], dq_ref.at[:, :, columns(start + p * HEAD)], dqs_sem.at[p], dqr_sem.at[p], partner
        )

    def results(p):
        here = pl.ds(p * HEAD, HEAD)
        return ((done.at[p, 0], dkv_ref.at[0, :, here]), (done.at[p, 1], dkv_ref.at[1, :, here]))

    def own_out(p, i):
        src, dst = results(p)[i]
        return local(src, dst, os_sem.at[p, i])

    def x_out(p, i):
        src, dst = results(p)[i]
        return remote(src, dst, os_sem.at[p, i], or_sem.at[p, i], partner)

    times = local(pos_ref, pos, pos_sem)
    times.start()
    for p in range(PLACES):
        own_k(p).start()
        own_v(p).start()
    barrier = pltpu.get_barrier_semaphore()

    def greet(peer):
        pl.semaphore_signal(barrier, inc=1, device_id=peer, device_id_type=MESH)

    greet(partner)
    greet(sibling)

    @pl.when(has_ahead)
    def _():
        greet(ahead)

    @pl.when(has_back)
    def _():
        greet(back)

    times.wait()
    small[0], small[1] = rope_tables(pos[...])
    cosines, sines = small[0], small[1]
    for p in range(PLACES):
        own_k(p).wait()
        raw = kraw[p].astype(jnp.float32)
        kv[p, 4, 0] = (raw * cosines + pltpu.roll(raw, HEAD // 2, 1) * sines).astype(jnp.bfloat16)
    for p in range(PLACES):
        own_v(p).wait()
    @pl.when(has_ahead & has_back)
    def _():
        pl.semaphore_wait(barrier, 4)

    @pl.when(first | last)
    def _():
        pl.semaphore_wait(barrier, 3)

    @pl.when(first)
    def _():
        for p in range(PLACES):
            kv[p, 0] = jnp.zeros((2, BLOCK, HEAD), jnp.bfloat16)
            kv[p, 2] = jnp.zeros((2, BLOCK, HEAD), jnp.bfloat16)

    @pl.when(last)
    def _():
        yin[...] = jnp.zeros(yin.shape, jnp.bfloat16)


    def send_own(p):
        @pl.when(has_ahead)
        def _():
            for kind in range(2):
                y_kv(p, 0, kind).start()

    send_own(0)
    send_own(1)
    for p in range(PLACES):
        x_q(p).start()
        x_g(p).start()
    for p in range(PLACES):
        own_q(p).start()
        own_g(p).start()

    def stage_a(p):
        for kind in range(2):
            @pl.when(has_back)
            def _():
                y_kv(p, 0, kind).wait_recv()

            @pl.when(has_ahead)
            def _():
                y_kv(p, 1, kind).start()

            c_kv(p, 0, kind).start()

        @pl.when(p + 2 < PLACES)
        def _():
            send_own(p + 2)

    def stage_b(p):
        for kind in range(2):
            @pl.when(has_back)
            def _():
                y_kv(p, 1, kind).wait_recv()

            c_kv(p, 1, kind).start()

    low = lax.broadcasted_iota(jnp.int32, (8, HEAD), 0) < 4
    for table in (0, 1):
        for pair in range(BLOCK // 2):
            first = jnp.broadcast_to(small[table, 2 * pair:2 * pair + 1, :], (8, HEAD))
            second = jnp.broadcast_to(small[table, 2 * pair + 1:2 * pair + 2, :], (8, HEAD))
            tab[table, 8 * pair:8 * pair + 8, :] = jnp.where(low, first, second)

    stage_a(0)
    for part in (0, 1):
        row = lax.broadcasted_iota(jnp.int32, (SPAN - 64, CHUNK), 0)
        token = lax.broadcasted_iota(jnp.int32, (SPAN - 64, CHUNK), 1) // groups
        allowed = (row > token) & (row <= token + BEHIND) & (block * BLOCK - BEHIND + 64 * part + row >= 0)
        bias[part] = jnp.where(allowed, 0.0, EXCLUDED).astype(jnp.float32)
    for low_precision in (ps, dss):
        for side in (0, 2 * CHUNK):
            low_precision[SPAN - 64:, side:side + CHUNK] = jnp.zeros((64, CHUNK), jnp.bfloat16)
            low_precision[:64, side + CHUNK:side + 2 * CHUNK] = jnp.zeros((64, CHUNK), jnp.bfloat16)
    stage_a(1)

    def rotate_queries(n, side):
        raw = qb[n].reshape(rows, HEAD).astype(jnp.float32)
        gr[side] = gb[n].reshape(rows, HEAD)
        qr[side] = (raw * tab[0] + pltpu.roll(raw, HEAD // 2, 1) * tab[1]).astype(jnp.bfloat16)

    own_q(0).wait()
    own_g(0).wait()
    rotate_queries(0, 0)
    stage_b(0)

    def weigh(p, n, side):
        keys = kv[p, :, 0].reshape(SPAN, HEAD)
        values = kv[p, :, 1].reshape(SPAN, HEAD)
        for part in (0, 1):
            here = slice(CHUNK * part, CHUNK * part + CHUNK)
            there = slice(rows * side + CHUNK * part, rows * side + CHUNK * part + CHUNK)
            seen = slice(64 * part, 64 * part + SPAN - 64)
            scores = lax.dot_general(keys[seen], qr[side, here], NT, preferred_element_type=jnp.float32) + bias[part]
            top = jnp.max(scores, 0, keepdims=True)
            raised = jnp.exp2((scores - top) * exponent_scale)
            weights = raised * (1.0 / jnp.sum(raised, 0, keepdims=True))
            grads = lax.dot_general(values[seen], gr[side, here], NT, preferred_element_type=jnp.float32)
            delta = jnp.sum(weights * grads, 0, keepdims=True)
            ps[seen, there] = weights.astype(jnp.bfloat16)
            dss[seen, there] = (weights * (grads - delta)).astype(jnp.bfloat16)

    def query_grads(n, side):
        query_part = dot(kt[...], dss[:, rows * side:rows * side + rows]).T
        query_part = query_part * score_scale
        rotated = query_part * tab[0] - pltpu.roll(query_part, HEAD // 2, 1) * tab[1]
        dqs[n] = rotated.astype(jnp.bfloat16).reshape(BLOCK, groups, HEAD)

    def key_grads(p):
        for kind, weights, vectors in ((1, ps, gr), (0, dss, qr)):
            acc[p, :, kind] = dot(weights[...], vectors[...].reshape(2 * rows, HEAD)).reshape(5, BLOCK, HEAD)
            for i in range(2):
                c_grad(p, i, kind).start()

    def combine_a(p):
        for kind in (1, 0):
            for i in range(2):
                c_grad(p, i, kind).wait_recv()
                acc[p, 4 - 2 * core - 2 * i, kind] += rin[p, i, kind]
            ysend[p, 1, kind] = acc[p, 0, kind].astype(jnp.bfloat16)

            @pl.when(has_back)
            def _():
                y_grad(p, 1, kind).start()

    def combine_b(p):
        for kind in (1, 0):
            @pl.when(has_ahead)
            def _():
                y_grad(p, 1, kind).wait_recv()

            ysend[p, 0, kind] = (acc[p, 2, kind] + yin[p, 1, kind].astype(jnp.float32)).astype(jnp.bfloat16)

            @pl.when(has_back)
            def _():
                y_grad(p, 0, kind).start()

    def total_of(p, kind):
        @pl.when(has_ahead)
        def _():
            y_grad(p, 0, kind).wait_recv()

        return acc[p, 4, kind] + yin[p, 0, kind].astype(jnp.float32)

    def finish(p, kind, total):
        if kind == 0:
            total = total * score_scale
            total = total * small[0] - pltpu.roll(total, HEAD // 2, 1) * small[1]
        done[p, kind] = total.astype(jnp.bfloat16)

    def finish_swapped(p):
        for kind in (1, 0):
            finish(p, kind, total_of(p, kind))

            @pl.when(flip == 0)
            def _():
                own_out(p, kind).start()

            @pl.when(flip == 1)
            def _():
                x_out(p, kind).start()

    @pl.loop(0, PLACES)
    def _(p):
        for i in range(2):
            for kind in range(2):
                c_kv(p, i, kind).wait_recv()
        kt[...] = kv[p, :, 0].reshape(SPAN, HEAD).T

        @pl.when(p + 2 < PLACES)
        def _():
            stage_a(p + 2)

        weigh(p, p, 0)
        query_grads(p, 0)
        own_dq(p).start()

        @pl.when(p + 1 < PLACES)
        def _():
            stage_b(p + 1)

        @pl.when(p > 0)
        def _():
            combine_a(p - 1)

        @pl.when(p > 1)
        def _():
            combine_b(p - 2)

        x_q(p).wait_recv()
        x_g(p).wait_recv()
        rotate_queries(PLACES + p, 1)
        weigh(p, PLACES + p, 1)
        key_grads(p)
        query_grads(PLACES + p, 1)
        x_dq(p, mine).start()

        @pl.when(p + 1 < PLACES)
        def _():
            own_q(p + 1).wait()
            own_g(p + 1).wait()
            rotate_queries(p + 1, 0)

    combine_b(PLACES - 2)
    combine_a(PLACES - 1)
    finish_swapped(0)
    finish_swapped(1)
    combine_b(PLACES - 1)
    finish_swapped(2)
    finish_swapped(3)

    @pl.when(has_ahead)
    def _():
        for p in range(PLACES):
            for i in range(2):
                for kind in range(2):
                    y_kv(p, i, kind).wait_send()

    @pl.when(has_back)
    def _():
        for p in range(PLACES):
            for i in range(2):
                for kind in range(2):
                    y_grad(p, i, kind).wait_send()

    for p in range(PLACES):
        own_dq(p).wait()
        for i in range(2):
            for kind in range(2):
                c_kv(p, i, kind).wait_send()
                c_grad(p, i, kind).wait_send()
    for p in range(PLACES):
        x_q(p).wait_send()
        x_g(p).wait_send()
        x_dq(p, mine).wait_send()
        x_dq(p, theirs).wait_recv()

    @pl.when(flip == 0)
    def _():
        for p in range(PLACES):
            for i in range(2):
                own_out(p, i).wait()

    @pl.when(flip == 1)
    def _():
        for p in range(PLACES):
            for i in range(2):
                x_out(p, i).wait_send()
                x_out(p, i).wait_recv()


def settle(dq_ref, dkv_ref, dq_out, dk_out, dv_out, dq_here, dkv_here, in_sem, out_sem):
    pieces = []
    step = dq_ref.shape[0] // SETTLE
    for n in range(SETTLE):
        rows = pl.ds(n * step, step)
        pieces.append((dq_ref.at[rows], dq_here.at[rows], dq_out.at[rows]))
    pieces.append((dkv_ref.at[0], dkv_here.at[0], dk_out))
    pieces.append((dkv_ref.at[1], dkv_here.at[1], dv_out))
    arrivals = [pltpu.make_async_copy(a, b, in_sem.at[n]) for n, (a, b, _) in enumerate(pieces)]
    leaves = [pltpu.make_async_copy(b, c, out_sem.at[n]) for n, (_, b, c) in enumerate(pieces)]
    for copy in arrivals:
        copy.start()
    for arrival, leave in zip(arrivals, leaves):
        arrival.wait()
        leave.start()
    for leave in leaves:
        leave.wait()


def body(outer_count, inner_count, queries, keys, values, grad_out, positions):
    tokens, groups, width = queries.shape
    rows = tokens * groups
    half = OWN_HEADS * HEAD
    low, high = jnp.bfloat16, jnp.float32
    semaphores = pltpu.SemaphoreType.DMA
    swapped = OWN_HEADS
    pairs = (PLACES, 2)
    anywhere = pl.BlockSpec(memory_space=pl.ANY)
    off_chip = pl.BlockSpec(memory_space=pltpu.HBM)
    dq, dkv = pl.pallas_call(
        functools.partial(kernel, outer_count, inner_count, groups),
        out_shape=(
            jax.ShapeDtypeStruct((tokens, groups, width), low),
            jax.ShapeDtypeStruct((2, tokens, half), low),
        ),
        in_specs=[anywhere] * 2 + [off_chip] * 3,
        out_specs=(anywhere, off_chip),
        scratch_shapes=[
            pltpu.VMEM((2 * OWN_HEADS, tokens, groups, HEAD), low),
            pltpu.VMEM((2 * OWN_HEADS, tokens, groups, HEAD), low),
            pltpu.VMEM((2, rows, HEAD), low),
            pltpu.VMEM((2, rows, HEAD), low),
            pltpu.VMEM((PLACES, tokens, HEAD), low),
            pltpu.VMEM((PLACES, 5, 2, BLOCK, HEAD), low),
            pltpu.VMEM((1, tokens), jnp.int32),
            pltpu.VMEM((2, tokens, HEAD), high),
            pltpu.VMEM((2, rows, HEAD), high),
            pltpu.VMEM((2, SPAN - 64, CHUNK), high),
            pltpu.VMEM((SPAN, 2 * rows), low),
            pltpu.VMEM((SPAN, 2 * rows), low),
            pltpu.VMEM((HEAD, SPAN), low),
            pltpu.VMEM((PLACES, 5, 2, BLOCK, HEAD), high),
            pltpu.VMEM((PLACES, 2, 2, BLOCK, HEAD), high),
            pltpu.VMEM((PLACES, 2, 2, BLOCK, HEAD), low),
            pltpu.VMEM((PLACES, 2, 2, BLOCK, HEAD), low),
            pltpu.VMEM((2 * OWN_HEADS, tokens, groups, HEAD), low),
            pltpu.VMEM((PLACES, 2, BLOCK, HEAD), low),
            semaphores,
            semaphores((PLACES,)),
            semaphores((PLACES,)),
            semaphores((PLACES,)),
            semaphores((PLACES,)),
            semaphores((2, swapped)),
            semaphores((2, swapped)),
            semaphores((PLACES, 4)),
            semaphores((PLACES, 4)),
            semaphores((PLACES, 4)),
            semaphores((PLACES, 4)),
            semaphores((PLACES, 4)),
            semaphores((PLACES, 4)),
            semaphores((PLACES, 4)),
            semaphores((PLACES, 4)),
            semaphores((PLACES,)),
            semaphores((swapped,)),
            semaphores((swapped,)),
            semaphores(pairs),
            semaphores(pairs),
        ],
        compiler_params=pltpu.CompilerParams(collective_id=0, has_side_effects=True, vmem_limit_bytes=62 * 2**20),
    )(
        queries,
        grad_out,
        keys,
        values,
        positions.reshape(1, tokens),
    )
    return pl.pallas_call(
        settle,
        out_shape=(
            jax.ShapeDtypeStruct((tokens, groups, width), low),
            jax.ShapeDtypeStruct((tokens, half), low),
            jax.ShapeDtypeStruct((tokens, half), low),
        ),
        in_specs=[off_chip] * 2,
        out_specs=(off_chip,) * 3,
        scratch_shapes=[
            pltpu.VMEM((tokens, groups, width), low),
            pltpu.VMEM((2, tokens, half), low),
            semaphores((SETTLE + 2,)),
            semaphores((SETTLE + 2,)),
        ],
        compiler_params=pltpu.CompilerParams(vmem_limit_bytes=62 * 2**20),
    )(dq, dkv)


def solution(mesh):
    placed = (
        P(("outer", "inner"), "head", None),
        P(("outer", "inner"), None),
        P(("outer", "inner"), None),
        P(("outer", "inner"), "head", None),
        P(("outer", "inner")),
    )
    return jax.shard_map(
        functools.partial(body, mesh.shape["outer"], mesh.shape["inner"]),
        mesh=mesh,
        in_specs=placed,
        out_specs=(
            P(("outer", "inner"), "head", None),
            P(("outer", "inner"), "head"),
            P(("outer", "inner"), "head"),
        ),
        check_vma=False,
    )
```

time: 65.7 us -> 56.6 us (0.86)
  local copies, waits for them, and re-layouts: 8.16 us -> 0 us
  other arithmetic: 0.97 us -> 0 us
    unnamed x18 -> x0, local copies, waits for them, and re-layouts: 5.28 us -> none
    reshape x3 -> x0, local copies, waits for them, and re-layouts: 2.88 us -> none  [the longest x1 1.43 us: body(): queries.reshape(rows, width)]
    pallas_call x0 -> x1, Pallas kernels: none -> 2.1 us  [body(): pl.pallas_call(settle, out_shape=(jax.ShapeDtypeStruct((tokens, groups, w...]
    pallas_call x1, Pallas kernels: 55.6 us -> 53.7 us  [body(): pl.pallas_call(functools.partial(kernel, outer_count, inner_count, groups...]
    convert_element_type x1 -> x0, other arithmetic: 0.66 us -> none  [rope_tables(): angles = positions.astype(jnp.float32)[:, None] * frequency[None, :]]
where the time goes in v3:
time: 56.6 us; the launch traced here: 56.4 us
  Pallas kernels  55.8 us (99%)
  between operations  0.64 us (1%)
    pallas_call x1, Pallas kernels, body(): pl.pallas_call(functools.partial(kernel, outer_count, inner_count, groups...  53.7 us
    pallas_call x1, Pallas kernels, body(): pl.pallas_call(settle, out_shape=(jax.ShapeDtypeStruct((tokens, groups, w...  2.1 us

profile of v3, /device:TPU:4, one launch (start us, length us, event | category | flops | bytes accessed | tf_op | source)
XLA Modules:
  0.0 56.4 jit_solution(10297512443920765493)
XLA Ops:
  0.6 53.7 %shard_map.76 = (bf16[128,4,1024]{2,1,0:T(4,128)(2,1)}, bf16[2,128,512]{2,1,0:T(8,128)(2,1)}) custom-call(bf16[128,4,1024]{2,1,0:T(4,128)(2,1)} %q_ref.1, bf16[128,4,1024]{2,1,0:T(4,128)(2,1)} %g_ref.1, bf16[128,1024]{1,0:T(8,128)(2,1)} %k_ref.1, bf16[128,1024]{1,0:T(8,128)(2,1)} %v_ref.1, s32[1,128]{1,0:T(1,128)} %bitcast.1), custom_call_target="tpu_custom_call" | custom-call | tf_op jit(solution)/shard_map/pallas_call | solution.py:477
  54.3 2.1 %shard_map.77 = (bf16[128,4,1024]{2,1,0:T(4,128)(2,1)}, bf16[128,512]{1,0:T(8,128)(2,1)}, bf16[128,512]{1,0:T(8,128)(2,1)}) custom-call(bf16[128,4,1024]{2,1,0:T(4,128)(2,1)} %get-tuple-element.5.dq_ref, bf16[2,128,512]{2,1,0:T(8,128)(2,1)} %get-tuple-element.6.dkv_ref), custom_call_target="tpu_custom_call" | custom-call | tf_op jit(solution)/shard_map/pallas_call | solution.py:534

commit v4 on v3

--- a/solution.py
+++ b/solution.py
@@ -128,20 +128,20 @@
 
     def y_kv(p, i, kind):
         n = 2 * i + kind
-        return remote(kv.at[p, 4 - 2 * i, kind], kv.at[p, 2 - 2 * i, kind], ys_sem.at[p, n], yr_sem.at[p, n], ahead)
+        return remote(kv.at[p, 4 - 2 * i, kind], kv.at[p, 2 - 2 * i, kind], ys_sem.at[p], yr_sem.at[p, n], ahead)
 
     def c_kv(p, i, kind):
         n = 2 * i + kind
         src = kv.at[p, 4 - 2 * core - 2 * i, kind]
-        return remote(src, kv.at[p, 3 - 2 * i, kind], cs_sem.at[p, n], cr_sem.at[p, n], sibling)
+        return remote(src, kv.at[p, 3 - 2 * i, kind], cs_sem.at[p], cr_sem.at[p, n], sibling)
 
     def c_grad(p, i, kind):
         n = 2 * i + kind
-        return remote(acc.at[p, 3 - 2 * i, kind], rin.at[p, i, kind], gcs_sem.at[p, n], gcr_sem.at[p, n], sibling)
+        return remote(acc.at[p, 3 - 2 * i, kind], rin.at[p, i, kind], gcs_sem.at[p], gcr_sem.at[p, n], sibling)
 
     def y_grad(p, i, kind):
         n = 2 * i + kind
-        return remote(ysend.at[p, i, kind], yin.at[p, i, kind], gys_sem.at[p, n], gyr_sem.at[p, n], back)
+        return remote(ysend.at[p, i, kind], yin.at[p, i, kind], gys_sem.at[p], gyr_sem.at[p, n], back)
 
     def own_dq(p):
         return local(dqs.at[p], dq_ref.at[:, :, columns(column_of(p))], dql_sem.at[p])
@@ -405,26 +405,25 @@
     finish_swapped(2)
     finish_swapped(3)
 
+    def sent(ref, p, sem, recv, device):
+        whole = ref.at[p, pl.ds(0, 2)]
+        remote(whole, whole, sem.at[p], recv.at[p, 0], device).wait_send()
+
     @pl.when(has_ahead)
     def _():
         for p in range(PLACES):
-            for i in range(2):
-                for kind in range(2):
-                    y_kv(p, i, kind).wait_send()
+            sent(kv, p, ys_sem, yr_sem, ahead)
 
     @pl.when(has_back)
     def _():
         for p in range(PLACES):
-            for i in range(2):
-                for kind in range(2):
-                    y_grad(p, i, kind).wait_send()
-
+            sent(ysend, p, gys_sem, gyr_sem, back)
+
+    for p in range(PLACES):
+        sent(kv, p, cs_sem, cr_sem, sibling)
+        sent(acc, p, gcs_sem, gcr_sem, sibling)
     for p in range(PLACES):
         own_dq(p).wait()
-        for i in range(2):
-            for kind in range(2):
-                c_kv(p, i, kind).wait_send()
-                c_grad(p, i, kind).wait_send()
     for p in range(PLACES):
         x_q(p).wait_send()
         x_g(p).wait_send()
@@ -509,13 +508,13 @@
             semaphores((PLACES,)),
             semaphores((2, swapped)),
             semaphores((2, swapped)),
+            semaphores((PLACES,)),
             semaphores((PLACES, 4)),
+            semaphores((PLACES,)),
             semaphores((PLACES, 4)),
+            semaphores((PLACES,)),
             semaphores((PLACES, 4)),
-            semaphores((PLACES, 4)),
-            semaphores((PLACES, 4)),
-            semaphores((PLACES, 4)),
-            semaphores((PLACES, 4)),
+            semaphores((PLACES,)),
             semaphores((PLACES, 4)),
             semaphores((PLACES,)),
             semaphores((swapped,)),

time: 56.6 us -> 56.2 us (level)
  no operation moved by 1% of the time
where the time goes in v4:
time: 56.2 us; the launch traced here: 56 us
  Pallas kernels  55.3 us (98%)
  between operations  0.64 us (1%)
    pallas_call x1, Pallas kernels, body(): pl.pallas_call(functools.partial(kernel, outer_count, inner_count, groups...  53.2 us
    pallas_call x1, Pallas kernels, body(): pl.pallas_call(settle, out_shape=(jax.ShapeDtypeStruct((tokens, groups, w...  2.1 us

profile of v4, /device:TPU:4, one launch (start us, length us, event | category | flops | bytes accessed | tf_op | source)
XLA Modules:
  0.0 56.0 jit_solution(14395709966173824764)
XLA Ops:
  0.6 53.2 %shard_map.76 = (bf16[128,4,1024]{2,1,0:T(4,128)(2,1)}, bf16[2,128,512]{2,1,0:T(8,128)(2,1)}) custom-call(bf16[128,4,1024]{2,1,0:T(4,128)(2,1)} %q_ref.1, bf16[128,4,1024]{2,1,0:T(4,128)(2,1)} %g_ref.1, bf16[128,1024]{1,0:T(8,128)(2,1)} %k_ref.1, bf16[128,1024]{1,0:T(8,128)(2,1)} %v_ref.1, s32[1,128]{1,0:T(1,128)} %bitcast.1), custom_call_target="tpu_custom_call" | custom-call | tf_op jit(solution)/shard_map/pallas_call | solution.py:476
  53.9 2.1 %shard_map.77 = (bf16[128,4,1024]{2,1,0:T(4,128)(2,1)}, bf16[128,512]{1,0:T(8,128)(2,1)}, bf16[128,512]{1,0:T(8,128)(2,1)}) custom-call(bf16[128,4,1024]{2,1,0:T(4,128)(2,1)} %get-tuple-element.5.dq_ref, bf16[2,128,512]{2,1,0:T(8,128)(2,1)} %get-tuple-element.6.dkv_ref), custom_call_target="tpu_custom_call" | custom-call | tf_op jit(solution)/shard_map/pallas_call | solution.py:533
